TPU v7x, 1024 devices: a whole 4x8x16 slice. The times are simulated.
1024 devices in a mesh: wide: 16 (over x_hi, y), narrow: 64 (over z, x_lo, core).
Axes of the slice: x: 4 (x_hi: 2, x_lo: 2; x = x_hi * 2 + x_lo), y: 8, z: 16, core: 2. Of those that a mesh axis runs over, the one named last changes fastest.
Arguments:
- pair_integrals: bfloat16 [65536, 1024], P(('wide', 'narrow')), may hold values from -0.01171875 to 0.01171875
- screening: bfloat16 [1024, 1024], replicated, may hold values from -0.1875 to 0.1875
- virtual_integrals: bfloat16 [1024, 1024, 1024], P(('wide', 'narrow')), may hold values from -0.75 to 0.75
- trials: bfloat16 [1, 256, 1024], P(None, None, 'narrow'), may hold values from -6 to 6
Outputs:
- response: float32 [1024, 1, 256], P('narrow', None, 'wide')
All inputs are finite; a program needn't handle non-finite values.
Results may differ from a plain program's by a relative error of at most 0.0041.
Values may be sent and summed in bfloat16 or wider, within the bound.
No kernel may reach another device: no remote copies, remote signals or barrier semaphores. Data moves between devices by JAX's collectives and lax.ppermute only.
A program may use at most 32 MiB of HBM per device.

v0:
```python
import jax
import jax.numpy as jnp
from jax import lax
from jax.sharding import PartitionSpec as P

O = 256


def per_device(pair_integrals, screening, virtual_integrals, trials):
    screened = jnp.dot(pair_integrals, screening, preferred_element_type=jnp.float32).astype(
        jnp.bfloat16
    )
    blocks = screened.reshape((1, 1) + screened.shape)
    owned_tiles = lax.all_to_all(
        lax.all_to_all(blocks, "wide", split_axis=3, concat_axis=0, tiled=True),
        "narrow",
        split_axis=3,
        concat_axis=1,
        tiled=True,
    )
    aux_here = owned_tiles.shape[3]
    pair_tiles = owned_tiles.reshape(O, O, aux_here)
    whole_trials = lax.all_gather(trials, "narrow", axis=2, tiled=True)
    halves = jnp.einsum(
        "qab,sjb->qasj", virtual_integrals, whole_trials, preferred_element_type=jnp.float32
    ).astype(jnp.bfloat16)
    shares = lax.psum_scatter(
        jnp.einsum("qasj,ijq->asi", halves, pair_tiles, preferred_element_type=jnp.float32),
        "narrow",
        scatter_dimension=0,
        tiled=True,
    )
    return lax.psum_scatter(shares, "wide", scatter_dimension=2, tiled=True)


def solution(mesh):
    return jax.shard_map(
        per_device,
        mesh=mesh,
        in_specs=(
            P(("wide", "narrow"), None),
            P(),
            P(("wide", "narrow"), None, None),
            P(None, None, "narrow"),
        ),
        out_specs=P("narrow", None, "wide"),
        check_vma=False,
    )
```

profile of v0, /device:TPU:1, one launch (start us, length us, event | category | flops | bytes accessed | tf_op | source)
XLA Modules:
  0.0 574.5 jit_solution(11307570928299796842)
XLA Ops:
  6.5 0.0 copy-start
  6.5 2.3 fusion.5
  8.8 0.4 copy.12
  9.2 0.5 broadcast
  9.7 0.0 copy-start.1
  9.7 2.3 reduce
  12.0 0.2 reshape.26
  12.3 18.9 %all_to_all.33 = bf16[16,2,2048]{2,1,0:T(2,128)(2,1)S(1)} all-to-all(bf16[16,2,2048]{2,1,0:T(2,128)(2,1)S(1)} %reshape.26), channel_id=1, replica_groups=mesh['wide'=16,'narrow'=64] {'wide'}, dimensions={0} | all-to-all | bytes 262144 | tf_op jit(solution)/shard_map/all_to_all | solution.py:15
  31.2 0.3 reshape.27
  31.5 0.3 copy.13
  31.9 0.2 all_to_all.25
  32.0 0.4 copy.14
  32.4 0.8 reshape.28
  33.3 21.4 %all-to-all-start.1 = ((bf16[64,2,512]{2,1,0:T(2,128)(2,1)}), bf16[64,2,512]{2,1,0:T(2,128)(2,1)S(1)}, u32[]{:S(2)}, u32[]{:S(2)}) async-start(bf16[64,2,512]{2,1,0:T(2,128)(2,1)} %reshape.28), calls=%async_computation.1 | async-start | bytes 262144 | tf_op jit(solution)/shard_map/all_to_all | solution.py:14
  54.7 0.0 reduce-scatter.5.cloned.1.call-start
  54.8 0.0 copy-done.1
  54.8 65.1 %all_gather.3 = bf16[1,256,1024]{1,2,0:T(8,128)(2,1)S(1)} all-gather(bf16[1,256,16]{1,2,0:T(8,128)(2,1)S(1)} %copy-done.1), channel_id=1, replica_groups=mesh['wide'=16,'narrow'=64] {'narrow'}, dimensions={2}, use_global_device_ids=true | all-gather | bytes 532480 | tf_op jit(solution)/shard_map/all_gather | solution.py:23
  119.8 0.0 all-to-all-done.1
  119.8 0.2 reshape.29
  120.1 0.1 copy.15
  120.2 0.2 reshape.23
  120.4 0.0 copy-done
  120.4 1.9 convolution_bitcast_fusion
  122.3 0.0 reduce-scatter.5.cloned.1.call-update
  122.4 0.0 reduce-scatter.7.cloned.1.call-start
  122.4 225.0 %reduce-scatter.5.cloned.1.call-done = f32[16,1,256]{2,0,1:T(8,128)} async-done(((f32[1024,1,256]{2,0,1:T(8,128)}), f32[16,1,256]{2,0,1:T(8,128)}) %reduce-scatter.5.cloned.1.call-update) | async-done | bytes 16400 | tf_op jit(solution)/shard_map/reduce_scatter | solution.py:27
  347.4 1.4 copy.17
  348.9 0.0 reduce-scatter.7.cloned.1.call-update
  348.9 217.4 %reduce-scatter.7.cloned.1.call-done = f32[16,16]{1,0:T(8,128)} async-done(((f32[256,16]{1,0:T(8,128)}), f32[16,16]{1,0:T(8,128)}) %reduce-scatter.7.cloned.1.call-update) | async-done | bytes 1040
  566.3 1.4 copy.18
  (1 shorter events, 0.0 us)
Async XLA Ops:
  6.5 113.8 %copy-start = (bf16[1,1024,1024]{2,1,0:T(8,128)(2,1)S(1)}, bf16[1,1024,1024]{2,1,0:T(8,128)(2,1)}, u32[]{:S(2)}) copy-start(bf16[1,1024,1024]{2,1,0:T(8,128)(2,1)} %param.6) | copy-start | bytes 6291460
  9.7 45.0 %copy-start.1 = (bf16[1,256,16]{1,2,0:T(8,128)(2,1)S(1)}, bf16[1,256,16]{1,2,0:T(8,128)(2,1)}, u32[]{:S(2)}) copy-start(bf16[1,256,16]{1,2,0:T(8,128)(2,1)} %param.7) | copy-start | bytes 24580
  33.3 86.6 %all-to-all-start.1 = ((bf16[64,2,512]{2,1,0:T(2,128)(2,1)}), bf16[64,2,512]{2,1,0:T(2,128)(2,1)S(1)}, u32[]{:S(2)}, u32[]{:S(2)}) async-start(bf16[64,2,512]{2,1,0:T(2,128)(2,1)} %reshape.28), calls=%async_computation.1 | async-start | bytes 262144 | tf_op jit(solution)/shard_map/all_to_all | solution.py:14
  54.7 292.7 %reduce-scatter.5.cloned.1.call-start = ((), (), s32[]{:S(2)}) async-start(), calls=%async_computation.4 | async-start | bytes 1064960 | tf_op jit(solution)/shard_map/reduce_scatter | solution.py:27
  122.4 443.9 %reduce-scatter.7.cloned.1.call-start = ((), (), s32[]{:S(2)}) async-start(), calls=%async_computation.5 | async-start | bytes 139264
Sparse Core Ops, SparseCore 0:
  122.5 224.8 reduce-scatter.4
  353.0 213.2 reduce-scatter.6
where the time goes:
time: 579 us; the launch traced here: 574 us
  waiting for transfers between devices  442 us (76%)
  blocking collectives  84 us (15%)
  starting transfers between devices  21.5 us (4%)
  between operations  13.5 us (2%)
  local copies, waits for them, and re-layouts  6.49 us (1%)
    reduce_scatter x1, waiting for transfers between devices, per_device(): lax.psum_scatter(jnp.einsum('qasj,ijq->asi', halves, pair_tiles, preferre...  225 us
    unnamed x3, waiting for transfers between devices  217 us
    all_gather x1, blocking collectives, per_device(): whole_trials = lax.all_gather(trials, 'narrow', axis=2, tiled=True)  65.1 us
    all_to_all x1, starting transfers between devices, per_device(): lax.all_to_all(lax.all_to_all(blocks, 'wide', split_axis=3, concat_axis=0...  21.4 us
    all_to_all x1, blocking collectives, per_device(): lax.all_to_all(blocks, 'wide', split_axis=3, concat_axis=0, tiled=True)  18.9 us
  transfers between devices with their start and end apart: 3, of which 2 were waited for; matrix products, arithmetic and copies ran while one was open for 0% of the time, Pallas kernels for 0%

commit v1 on v0

v1 whole, which is shorter than its diff:
```python
import jax
import jax.numpy as jnp
from jax import lax
from jax.experimental import pallas as pl
from jax.experimental.pallas import tpu as pltpu
from jax.sharding import PartitionSpec as P

O = 256
V = 1024
W = 16
N = 64
BLK = 16
BF = jnp.bfloat16
F32 = jnp.float32


def iota(shape, axis):
    return lax.broadcasted_iota(jnp.int32, shape, axis)


def picks(mask):
    return jnp.where(mask, 1.0, 0.0).astype(BF)


def dot(a, b, ca, cb):
    return lax.dot_general(a, b, (((ca,), (cb,)), ((), ())), preferred_element_type=F32)


def first_messages(wide_at, pairs, screening, trials):
    screened = dot(pairs, screening, 1, 0)
    columns = screened.T.astype(BF)
    tile_of = picks(iota((O, O), 0) == wide_at * BLK + iota((O, O), 1) // BLK)
    spread = dot(trials, tile_of, 1, 0)
    row = jnp.sum(jnp.where(iota((BLK, O), 0) == iota((BLK, O), 1) % BLK, spread, 0.0), 0, keepdims=True)
    parts = [columns[N * w : N * (w + 1), :] for w in range(W)]
    return jnp.concatenate(parts + [jnp.broadcast_to(row, (N, O)).astype(BF)], 1)


def second_messages(got):
    order = picks(iota((N, N), 1) == (iota((N, N), 0) % BLK) * 4 + iota((N, N), 0) // BLK)
    tiles = dot(order, got[:, :V], 1, 0)
    left = iota((BLK, 128), 1) < 64
    blocks = []
    for k in range(W // 2):
        t = [tiles[BLK * j : BLK * (j + 1), 128 * k : 128 * (k + 1)] for j in range(4)]
        r = [pltpu.roll(u, 64, 1) for u in t]
        even = [jnp.where(left, t[0], r[1]), jnp.where(left, t[2], r[3])]
        odd = [jnp.where(left, r[0], t[1]), jnp.where(left, r[2], t[3])]
        blocks += [jnp.concatenate(even, 1).astype(BF), jnp.concatenate(odd, 1).astype(BF)]
    rows = dot(picks(iota((V, N), 0) // BLK == iota((V, N), 1)), got[:, V:], 1, 0)
    kept = jnp.where(iota((V, O), 0) % BLK == iota((V, O), 1) % BLK, rows, 0.0).astype(BF)
    trials = dot(picks(iota((BLK, O), 0) == iota((BLK, O), 1) // BLK), kept, 1, 1).astype(BF)
    return blocks, trials


def third_messages(got):
    total = jnp.sum(got.astype(F32), 0).astype(BF)
    rows = dot(total, picks(iota((BLK, O), 0) == iota((BLK, O), 1) % BLK), 0, 0)
    kept = jnp.where(iota((V, O), 0) % BLK == iota((V, O), 1) // BLK, rows, 0.0).astype(BF)
    return dot(picks(iota((N, V), 0) == iota((N, V), 1) // BLK), kept, 1, 0).astype(BF)


def last_sum(got):
    total = jnp.sum(got.astype(F32), 0, keepdims=True)
    rows = jnp.where(iota((BLK, O), 0) == iota((BLK, O), 1) // BLK, total, 0.0)
    lanes = jnp.where(iota((O, BLK), 0) % BLK == iota((O, BLK), 1), 1.0, 0.0)
    return lax.dot_general(
        rows, lanes, (((1,), (0,)), ((), ())), precision=lax.Precision.HIGHEST, preferred_element_type=F32
    )


def store_pairs(ref, rows):
    half = rows.shape[1] // 2
    ref[:, 0, :] = rows[:, :half]
    ref[:, 1, :] = rows[:, half:]


def load_pairs(ref):
    return jnp.concatenate([ref[:, 0, :], ref[:, 1, :]], 1)


def first_kernel(wide_ref, pairs_ref, screening_ref, trials_ref, out_ref):
    store_pairs(out_ref, first_messages(wide_ref[0], pairs_ref[...], screening_ref[...], trials_ref[...]))


def second_kernel(got_ref, out_ref):
    blocks, trials = second_messages(load_pairs(got_ref))
    for w in range(W):
        out_ref[w, :, :O] = blocks[w]
        out_ref[w, :, O:] = trials


def third_kernel(got_ref, out_ref):
    store_pairs(out_ref, third_messages(got_ref[...]))


def last_kernel(got_ref, out_ref):
    out_ref[...] = last_sum(load_pairs(got_ref)).reshape(BLK, 1, BLK)


def call(body, shape, dtype, *args):
    specs = [pl.BlockSpec(memory_space=pltpu.VMEM)] * len(args)
    if args[0].dtype == jnp.int32:
        specs[0] = pl.BlockSpec(memory_space=pltpu.SMEM)
    return pl.pallas_call(
        body,
        out_shape=jax.ShapeDtypeStruct(shape, dtype),
        in_specs=specs,
        out_specs=pl.BlockSpec(memory_space=pltpu.VMEM),
        name=body.__name__,
    )(*args)


def swap(v, axis):
    return lax.all_to_all(v, axis, 0, 0, tiled=True)


def per_device(pair_integrals, screening, virtual_integrals, trials):
    wide_at = lax.axis_index("wide").reshape(1).astype(jnp.int32)
    mine = trials.reshape(O, BLK).T
    got = swap(call(first_kernel, (N, 2, (V + O) // 2), BF, wide_at, pair_integrals, screening, mine), "narrow")
    got = swap(call(second_kernel, (W, BLK, O + V), BF, got), "wide").reshape(O, O + V)
    halves = dot(virtual_integrals.reshape(V, V), got[:, O:], 1, 1).astype(BF)
    partial = dot(got[:, :O], halves, 1, 1).astype(BF)
    got = swap(partial.reshape(W, BLK, V), "wide")
    got = swap(call(third_kernel, (N, 2, O // 2), BF, got), "narrow")
    return call(last_kernel, (BLK, 1, BLK), F32, got)


def solution(mesh):
    return jax.shard_map(
        per_device,
        mesh=mesh,
        in_specs=(
            P(("wide", "narrow"), None),
            P(),
            P(("wide", "narrow"), None, None),
            P(None, None, "narrow"),
        ),
        out_specs=P("narrow", None, "wide"),
        check_vma=False,
    )
```

time: 579 us -> 121 us (0.21)
  waiting for transfers between devices: 442 us -> 0 us
  blocking collectives: 84 us -> 110 us
  starting transfers between devices: 21.5 us -> 0 us
  between operations: 13.5 us -> 0.01 us
  Pallas kernels: 0 us -> 9.69 us
  local copies, waits for them, and re-layouts: 6.49 us -> 0.01 us
    reduce_scatter x1 -> x0, waiting for transfers between devices: 225 us -> none  [per_device(): lax.psum_scatter(jnp.einsum('qasj,ijq->asi', halves, pair_tiles, preferre...]
    unnamed x3 -> x0, waiting for transfers between devices: 217 us -> none
    all_to_all x1 -> x4, blocking collectives: 18.9 us -> 110 us  [swap(): return lax.all_to_all(v, axis, 0, 0, tiled=True)]
    all_gather x1 -> x0, blocking collectives: 65.1 us -> none  [per_device(): whole_trials = lax.all_gather(trials, 'narrow', axis=2, tiled=True)]
    all_to_all x1 -> x0, starting transfers between devices: 21.4 us -> none  [per_device(): lax.all_to_all(lax.all_to_all(blocks, 'wide', split_axis=3, concat_axis=0...]
    pallas_call x0 -> x4, Pallas kernels: none -> 9.69 us  [call(): pl.pallas_call(body, out_shape=jax.ShapeDtypeStruct(shape, dtype), in_spe...]
  transfers between devices with their start and end apart: 3 -> 0, of which waited for: 2 -> 0; matrix products, arithmetic and copies ran while one was open for 0% -> 0% of each run, Pallas kernels for 0% -> 0%
where the time goes in v1:
time: 121 us; the launch traced here: 120 us
  blocking collectives  110 us (91%)
  Pallas kernels  9.69 us (8%)
    all_to_all x4, blocking collectives, swap(): return lax.all_to_all(v, axis, 0, 0, tiled=True)  110 us
    pallas_call x4, Pallas kernels, call(): pl.pallas_call(body, out_shape=jax.ShapeDtypeStruct(shape, dtype), in_spe...  9.69 us

profile of v1, /device:TPU:1, one launch (start us, length us, event | category | flops | bytes accessed | tf_op | source)
XLA Modules:
  0.0 120.3 jit_solution(3051982689342721514)
XLA Ops:
  0.0 0.0 copy-start
  0.0 3.1 %first_kernel.1 = bf16[64,2,640]{2,1,0:T(2,128)(2,1)} custom-call(s32[1]{0:T(128)} %bitcast.wide_ref, bf16[64,1024]{1,0:T(8,128)(2,1)} %pairs_ref.1, bf16[1024,1024]{1,0:T(8,128)(2,1)} %screening_ref.1, bf16[16,256]{1,0:T(8,128)(2,1)} %bitcast.15), custom_call_target="tpu_custom_call" | custom-call | tf_op jit(solution)/shard_map/first_kernel/pallas_call | solution.py:105
  3.1 40.1 %all_to_all.20.got_ref = bf16[64,2,640]{2,1,0:T(2,128)(2,1)} all-to-all(bf16[64,2,640]{2,1,0:T(2,128)(2,1)} %first_kernel.1), channel_id=1, replica_groups=mesh['wide'=16,'narrow'=64] {'narrow'}, dimensions={0} | all-to-all | bytes 327680 | tf_op jit(solution)/shard_map/all_to_all | solution.py:115
  43.2 2.6 %second_kernel.1 = bf16[16,16,1280]{2,1,0:T(8,128)(2,1)} custom-call(bf16[64,2,640]{2,1,0:T(2,128)(2,1)} %all_to_all.20.got_ref), custom_call_target="tpu_custom_call" | custom-call | tf_op jit(solution)/shard_map/second_kernel/pallas_call | solution.py:105
  45.8 27.9 %all_to_all.21 = bf16[16,16,1280]{2,1,0:T(8,128)(2,1)S(1)} all-to-all(bf16[16,16,1280]{2,1,0:T(8,128)(2,1)} %second_kernel.1), channel_id=1, replica_groups=mesh['wide'=16,'narrow'=64] {'wide'}, dimensions={0} | all-to-all | bytes 1310720 | tf_op jit(solution)/shard_map/all_to_all | solution.py:115
  73.7 0.0 copy-done
  73.7 1.0 convolution_convert_fusion
  74.7 20.1 %all_to_all.22.got_ref = bf16[16,16,1024]{2,1,0:T(8,128)(2,1)} all-to-all(bf16[16,16,1024]{2,1,0:T(8,128)(2,1)S(1)} %bitcast.14), channel_id=1, replica_groups=mesh['wide'=16,'narrow'=64] {'wide'}, dimensions={0} | all-to-all | bytes 1048576 | tf_op jit(solution)/shard_map/all_to_all | solution.py:115
  94.8 2.3 %third_kernel.1 = bf16[64,2,128]{2,1,0:T(2,128)(2,1)} custom-call(bf16[16,16,1024]{2,1,0:T(8,128)(2,1)} %all_to_all.22.got_ref), custom_call_target="tpu_custom_call" | custom-call | tf_op jit(solution)/shard_map/third_kernel/pallas_call | solution.py:105
  97.1 21.6 %all_to_all.23.got_ref = bf16[64,2,128]{2,1,0:T(2,128)(2,1)} all-to-all(bf16[64,2,128]{2,1,0:T(2,128)(2,1)} %third_kernel.1), channel_id=1, replica_groups=mesh['wide'=16,'narrow'=64] {'narrow'}, dimensions={0} | all-to-all | bytes 65536 | tf_op jit(solution)/shard_map/all_to_all | solution.py:115
  118.6 1.7 %last_kernel.1 = f32[16,1,16]{2,1,0:T(1,128)} custom-call(bf16[64,2,128]{2,1,0:T(2,128)(2,1)} %all_to_all.23.got_ref), custom_call_target="tpu_custom_call" | custom-call | tf_op jit(solution)/shard_map/last_kernel/pallas_call | solution.py:105
Async XLA Ops:
  0.0 73.7 %copy-start = (bf16[1,1024,1024]{2,1,0:T(8,128)(2,1)S(1)}, bf16[1,1024,1024]{2,1,0:T(8,128)(2,1)}, u32[]{:S(2)}) copy-start(bf16[1,1024,1024]{2,1,0:T(8,128)(2,1)} %param.6) | copy-start | bytes 6291460

commit v2 on v1

--- a/solution.py
+++ b/solution.py
@@ -98,17 +98,21 @@
     out_ref[...] = last_sum(load_pairs(got_ref)).reshape(BLK, 1, BLK)
 
 
+def in_vmem(v):
+    return pltpu.with_memory_space_constraint(v, pltpu.VMEM)
+
+
 def call(body, shape, dtype, *args):
     specs = [pl.BlockSpec(memory_space=pltpu.VMEM)] * len(args)
     if args[0].dtype == jnp.int32:
         specs[0] = pl.BlockSpec(memory_space=pltpu.SMEM)
     return pl.pallas_call(
         body,
-        out_shape=jax.ShapeDtypeStruct(shape, dtype),
+        out_shape=pltpu.VMEM(shape, dtype) if body is not last_kernel else jax.ShapeDtypeStruct(shape, dtype),
         in_specs=specs,
         out_specs=pl.BlockSpec(memory_space=pltpu.VMEM),
         name=body.__name__,
-    )(*args)
+    )(*[in_vmem(a) if body is not first_kernel else a for a in args])
 
 
 def swap(v, axis):

time: 121 us -> 114 us (0.942)
  Pallas kernels: 9.69 us -> 4.84 us
  blocking collectives: 110 us -> 108 us
    pallas_call x4, Pallas kernels: 9.69 us -> 4.84 us  [call(): pl.pallas_call(body, out_shape=pltpu.VMEM(shape, dtype) if body is not la...]
    all_to_all x4, blocking collectives: 110 us -> 108 us  [swap(): return lax.all_to_all(v, axis, 0, 0, tiled=True)]
where the time goes in v2:
time: 114 us; the launch traced here: 113 us
  blocking collectives  108 us (95%)
  Pallas kernels  4.84 us (4%)
    all_to_all x4, blocking collectives, swap(): return lax.all_to_all(v, axis, 0, 0, tiled=True)  108 us
    pallas_call x4, Pallas kernels, call(): pl.pallas_call(body, out_shape=pltpu.VMEM(shape, dtype) if body is not la...  4.84 us

profile of v2, /device:TPU:1, one launch (start us, length us, event | category | flops | bytes accessed | tf_op | source)
XLA Modules:
  0.0 113.5 jit_solution(4430984449728671315)
XLA Ops:
  0.0 0.0 copy-start
  0.0 2.4 %first_kernel.1 = bf16[64,2,640]{2,1,0:T(2,128)(2,1)S(1)} custom-call(s32[1]{0:T(128)} %bitcast.wide_ref, bf16[64,1024]{1,0:T(8,128)(2,1)} %pairs_ref.1, bf16[1024,1024]{1,0:T(8,128)(2,1)} %screening_ref.1, bf16[16,256]{1,0:T(8,128)(2,1)} %bitcast.15), custom_call_target="tpu_custom_call" | custom-call | tf_op jit(solution)/shard_map/first_kernel/pallas_call | solution.py:109
  2.5 39.8 %all_to_all.20.got_ref = bf16[64,2,640]{2,1,0:T(2,128)(2,1)S(1)} all-to-all(bf16[64,2,640]{2,1,0:T(2,128)(2,1)S(1)} %first_kernel.1), channel_id=1, replica_groups=mesh['wide'=16,'narrow'=64] {'narrow'}, dimensions={0} | all-to-all | bytes 327680 | tf_op jit(solution)/shard_map/all_to_all | solution.py:119
  42.2 0.9 second_kernel.1
  43.1 27.7 %all_to_all.21 = bf16[16,16,1280]{2,1,0:T(8,128)(2,1)S(1)} all-to-all(bf16[16,16,1280]{2,1,0:T(8,128)(2,1)S(1)} %second_kernel.1), channel_id=1, replica_groups=mesh['wide'=16,'narrow'=64] {'wide'}, dimensions={0} | all-to-all | bytes 1310720 | tf_op jit(solution)/shard_map/all_to_all | solution.py:119
  70.8 0.0 copy-done
  70.8 1.0 convolution_convert_fusion
  71.8 20.6 %all_to_all.22.got_ref = bf16[16,16,1024]{2,1,0:T(8,128)(2,1)S(1)} all-to-all(bf16[16,16,1024]{2,1,0:T(8,128)(2,1)S(1)} %bitcast.14), channel_id=1, replica_groups=mesh['wide'=16,'narrow'=64] {'wide'}, dimensions={0} | all-to-all | bytes 1048576 | tf_op jit(solution)/shard_map/all_to_all | solution.py:119
  92.4 0.6 third_kernel.1
  93.0 19.5 %all_to_all.23.got_ref = bf16[64,2,128]{2,1,0:T(2,128)(2,1)S(1)} all-to-all(bf16[64,2,128]{2,1,0:T(2,128)(2,1)S(1)} %third_kernel.1), channel_id=1, replica_groups=mesh['wide'=16,'narrow'=64] {'narrow'}, dimensions={0} | all-to-all | bytes 65536 | tf_op jit(solution)/shard_map/all_to_all | solution.py:119
  112.6 0.9 last_kernel.1
Async XLA Ops:
  0.0 70.8 %copy-start = (bf16[1,1024,1024]{2,1,0:T(8,128)(2,1)S(1)}, bf16[1,1024,1024]{2,1,0:T(8,128)(2,1)}, u32[]{:S(2)}) copy-start(bf16[1,1024,1024]{2,1,0:T(8,128)(2,1)} %param.6) | copy-start | bytes 6291460

commit v3 on v0

v3 whole, which is shorter than its diff:
```python
import jax
import jax.numpy as jnp
from jax import lax
from jax.experimental import pallas as pl
from jax.experimental.pallas import tpu as pltpu
from jax.sharding import Mesh, PartitionSpec as P

O = 256
V = 1024
W = 16
Z = 16
BLK = 16
XY = ("xh", "y", "xl")
ALL = ("xh", "y", "z", "xl", "c")
BF = jnp.bfloat16
F32 = jnp.float32


def iota(shape, axis):
    return lax.broadcasted_iota(jnp.int32, shape, axis)


def ones_at(mask, dtype=BF):
    return jnp.where(mask, 1.0, 0.0).astype(dtype)


def dot(a, b, ca, cb, precision=None):
    return lax.dot_general(
        a, b, (((ca,), (cb,)), ((), ())), precision=precision, preferred_element_type=F32
    )


def first_kernel(at_ref, pairs_ref, screening_ref, trials_ref, out_ref, columns_ref):
    columns_ref[...] = dot(pairs_ref[...], screening_ref[...], 1, 0).T
    mine = iota((BLK, O), 0) == at_ref[0]
    row = jnp.sum(jnp.where(mine, trials_ref[...].astype(F32), 0.0), 0, keepdims=True)
    rank = iota((8, 128), 0)
    tail = jnp.where(rank == 0, row[:, :128], jnp.where(rank == 1, row[:, 128:], 0.0)).astype(BF)
    for z in range(Z):
        for x in range(2):
            left, right = (columns_ref[pl.ds(4 * z + 2 * x + c, W, 64), :] for c in range(2))
            out_ref[z, W * x : W * (x + 1), :] = jnp.concatenate([left, right], 1).astype(BF)
        out_ref[z, 32:, :] = tail


def second_kernel(got_ref, out_ref, rows_ref):
    rows_ref[...] = got_ref[...].reshape(Z * 40, 128).astype(F32)
    trials = jnp.concatenate([rows_ref[pl.ds(r, Z, 40), :] for r in (32, 33)], 1).astype(BF)
    for w in range(W):
        for x in range(2):
            out_ref[2 * w + x, :, :128] = rows_ref[pl.ds(W * x + w, Z, 40), :].astype(BF)
            out_ref[2 * w + x, :, 128:] = trials


def third_kernel(at_ref, own_ref, other_ref, virtual_ref, send_ref, keep_ref, screened_ref, trials_ref):
    core = at_ref[0]
    here = iota((BLK, 128), 1) // 64 == core
    for w in range(W):
        for x in range(2):
            moved = pltpu.roll(other_ref[2 * w + x, :, :128].astype(F32), 64, 1)
            tile = jnp.where(here, own_ref[2 * w + x, :, :128].astype(F32), moved)
            screened_ref[BLK * w : BLK * (w + 1), 128 * x : 128 * (x + 1)] = tile.astype(BF)
    flip = ones_at(iota((O, O), 1) == iota((O, O), 0) % W * Z + iota((O, O), 0) // W)
    for x in range(2):
        for ref, c in ((own_ref, core), (other_ref, 1 - core)):
            tile = jnp.concatenate([ref[2 * w + x, :, 128:] for w in range(W)], 0)
            tile = dot(flip, tile, 1, 0).astype(BF)
            for z in range(Z):
                start = pl.multiple_of(64 * z + 32 * x + BLK * c, BLK)
                trials_ref[pl.ds(start, BLK), :] = tile[W * z : W * (z + 1), :]
    for ref, c in ((send_ref, 1 - core), (keep_ref, core)):
        for x in range(2):
            rows = virtual_ref[:, 2 * x + c].reshape(O, V)
            halves = dot(rows, trials_ref[...], 1, 0).astype(BF)
            part = dot(screened_ref[...], halves, 1, 1).astype(ref.dtype)
            for w in range(W):
                ref[2 * w + x] = part[BLK * w : BLK * (w + 1), :]


def add_kernel(kept_ref, got_ref, out_ref):
    out_ref[...] = (kept_ref[...] + got_ref[...].astype(F32)).astype(BF)


def fourth_kernel(got_ref, out_ref):
    total = jnp.sum(got_ref[...].astype(F32), 0)
    full = lax.Precision.HIGHEST
    rows = dot(total, ones_at(iota((BLK, O), 0) == iota((BLK, O), 1) % BLK, F32), 0, 0, full)
    kept = jnp.where(iota((O, O), 0) % BLK == iota((O, O), 1) // BLK, rows, 0.0)
    tiles = dot(ones_at(iota((Z, O), 0) == iota((Z, O), 1) // BLK, F32), kept, 1, 0, full)
    out_ref[:, 0, :] = tiles[:, :128]
    out_ref[:, 1, :] = tiles[:, 128:]


def last_kernel(got_ref, out_ref):
    total = jnp.sum(jnp.concatenate([got_ref[:, 0, :], got_ref[:, 1, :]], 1), 0, keepdims=True)
    rows = jnp.where(iota((BLK, O), 0) == iota((BLK, O), 1) // BLK, total, 0.0)
    lanes = ones_at(iota((O, BLK), 0) % BLK == iota((O, BLK), 1), F32)
    out_ref[...] = dot(rows, lanes, 1, 0, lax.Precision.HIGHEST).reshape(BLK, 1, BLK)


def in_vmem(v):
    return pltpu.with_memory_space_constraint(v, pltpu.VMEM)


def vmem_out(shape, dtype):
    return pltpu.VMEM(shape, dtype)


def call(body, outs, *args, scratch=(), limit=24 << 20):
    vmem = pl.BlockSpec(memory_space=pltpu.VMEM)
    specs = [pl.BlockSpec(memory_space=pltpu.SMEM) if a.dtype == jnp.int32 else vmem for a in args]
    return pl.pallas_call(
        body,
        out_shape=outs,
        in_specs=specs,
        out_specs=jax.tree.map(lambda o: vmem, outs),
        scratch_shapes=scratch,
        compiler_params=pltpu.CompilerParams(vmem_limit_bytes=limit),
        name=body.__name__,
    )(*args)


def swap(v, axis):
    return in_vmem(lax.all_to_all(v, axis, 0, 0, tiled=True))


def across(v):
    return in_vmem(lax.ppermute(v, "c", [(0, 1), (1, 0)]))


def per_device(pair_integrals, screening, virtual_integrals, trials):
    at = lax.axis_index(("xh", "y")).reshape(1).astype(jnp.int32)
    core = lax.axis_index("c").reshape(1).astype(jnp.int32)
    sent = call(
        first_kernel,
        vmem_out((Z, 40, 128), BF),
        at,
        pair_integrals,
        screening,
        trials.reshape(O, BLK).T,
        scratch=[pltpu.VMEM((V, 64), F32)],
        limit=None,
    )
    got = swap(sent, "z")
    sent = call(second_kernel, vmem_out((2 * W, Z, 384), BF), got, scratch=[pltpu.VMEM((Z * 40, 128), F32)])
    own = swap(sent, XY)
    sent, kept = call(
        third_kernel,
        (vmem_out((2 * W, BLK, O), BF), vmem_out((2 * W, BLK, O), F32)),
        core,
        own,
        across(own),
        in_vmem(virtual_integrals.reshape(Z, 4, BLK, V)),
        scratch=[pltpu.VMEM((O, O), BF), pltpu.VMEM((V, O), BF)],
    )
    got = swap(call(add_kernel, vmem_out((2 * W, BLK, O), BF), kept, across(sent)), XY)
    got = swap(call(fourth_kernel, vmem_out((Z, 2, 128), F32), got), "z")
    return call(last_kernel, jax.ShapeDtypeStruct((BLK, 1, BLK), F32), got)


def solution(mesh):
    chips = Mesh(mesh.devices.reshape(2, 8, 16, 2, 2), ALL)
    return jax.shard_map(
        per_device,
        mesh=chips,
        in_specs=(
            P(ALL, None),
            P(),
            P(ALL, None, None),
            P(None, None, ("z", "xl", "c")),
        ),
        out_specs=P(("z", "xl", "c"), None, ("xh", "y")),
        check_vma=False,
    )
```

time: 579 us -> 108 us (0.19)
  waiting for transfers between devices: 442 us -> 2.46 us
  between operations: 13.5 us -> 0.05 us
  starting transfers between devices: 21.5 us -> 9.94 us
  Pallas kernels: 0 us -> 6.65 us
  local copies, waits for them, and re-layouts: 6.49 us -> 0.01 us
    reduce_scatter x1 -> x0, waiting for transfers between devices: 225 us -> none  [per_device(): lax.psum_scatter(jnp.einsum('qasj,ijq->asi', halves, pair_tiles, preferre...]
    unnamed x3 -> x0, waiting for transfers between devices: 217 us -> none
    all_to_all x1 -> x4, blocking collectives: 18.9 us -> 87.4 us  [swap(): return in_vmem(lax.all_to_all(v, axis, 0, 0, tiled=True))]
    all_gather x1 -> x0, blocking collectives: 65.1 us -> none  [per_device(): whole_trials = lax.all_gather(trials, 'narrow', axis=2, tiled=True)]
    all_to_all x1 -> x0, starting transfers between devices: 21.4 us -> none  [per_device(): lax.all_to_all(lax.all_to_all(blocks, 'wide', split_axis=3, concat_axis=0...]
    ppermute x0 -> x2, starting transfers between devices: none -> 9.94 us  [across(): return in_vmem(lax.ppermute(v, 'c', [(0, 1), (1, 0)]))]
    pallas_call x0 -> x6, Pallas kernels: none -> 6.65 us  [call(): pl.pallas_call(body, out_shape=outs, in_specs=specs, out_specs=jax.tree.m...]
  transfers between devices with their start and end apart: 3 -> 2, of which waited for: 2 -> 2; matrix products, arithmetic and copies ran while one was open for 0% -> 0% of each run, Pallas kernels for 0% -> 0%
where the time goes in v3:
time: 108 us; the launch traced here: 106 us
  blocking collectives  87.4 us (81%)
  starting transfers between devices  9.94 us (9%)
  Pallas kernels  6.65 us (6%)
  waiting for transfers between devices  2.46 us (2%)
    all_to_all x4, blocking collectives, swap(): return in_vmem(lax.all_to_all(v, axis, 0, 0, tiled=True))  87.4 us
    ppermute x2, starting transfers between devices, across(): return in_vmem(lax.ppermute(v, 'c', [(0, 1), (1, 0)]))  9.94 us
    pallas_call x6, Pallas kernels, call(): pl.pallas_call(body, out_shape=outs, in_specs=specs, out_specs=jax.tree.m...  6.65 us
    ppermute x2, waiting for transfers between devices, across(): return in_vmem(lax.ppermute(v, 'c', [(0, 1), (1, 0)]))  2.46 us
  transfers between devices with their start and end apart: 2, of which 2 were waited for; matrix products, arithmetic and copies ran while one was open for 0% of the time, Pallas kernels for 0%

profile of v3, /device:TPU:1, one launch (start us, length us, event | category | flops | bytes accessed | tf_op | source)
XLA Modules:
  0.0 106.5 jit_solution(2748985515000217370)
XLA Ops:
  0.0 0.0 copy-start
  0.0 2.6 %first_kernel.1 = bf16[16,40,128]{2,1,0:T(8,128)(2,1)S(1)} custom-call(s32[1]{0:T(128)} %bitcast.1.at_ref, bf16[64,1024]{1,0:T(8,128)(2,1)} %pairs_ref.1, bf16[1024,1024]{1,0:T(8,128)(2,1)} %screening_ref.1, bf16[16,256]{1,0:T(8,128)(2,1)} %bitcast.7), custom_call_target="tpu_custom_call" | custom-call | tf_op jit(solution)/shard_map/first_kernel/pallas_call | solution.py:112
  2.6 31.4 %all_to_all.20.got_ref = bf16[16,40,128]{2,1,0:T(8,128)(2,1)S(1)} all-to-all(bf16[16,40,128]{2,1,0:T(8,128)(2,1)S(1)} %first_kernel.1), channel_id=1, replica_groups=mesh['xh'=2,'y'=8,'z'=16,'xl'=2,'c'=2] {'z'}, dimensions={0} | all-to-all | bytes 327680 | tf_op jit(solution)/shard_map/all_to_all | solution.py:124
  34.0 0.1 second_kernel.1
  34.0 22.1 %all_to_all.21.own_ref = bf16[32,16,384]{2,1,0:T(8,128)(2,1)S(1)} all-to-all(bf16[32,16,384]{2,1,0:T(8,128)(2,1)S(1)} %second_kernel.1), channel_id=1, replica_groups=mesh['xh'=2,'y'=8,'z'=16,'xl'=2,'c'=2] {'xh','y','xl'}, dimensions={0} | all-to-all | bytes 786432 | tf_op jit(solution)/shard_map/all_to_all | solution.py:124
  56.1 7.7 %collective-permute-start = (bf16[32,16,384]{2,1,0:T(8,128)(2,1)S(1)}, bf16[32,16,384]{2,1,0:T(8,128)(2,1)S(1)}, u32[]{:S(2)}, u32[]{:S(2)}) collective-permute-start(bf16[32,16,384]{2,1,0:T(8,128)(2,1)S(1)} %all_to_all.21.own_ref), channel_id=1, source_target_pairs={{0,1},{1,0},{2,3},{3,2},{4,5},{5,4},{6,7},{7,6},{8,9},{9,8},{10,11... | collective-permute-start | bytes 1179656 | tf_op jit(solution)/shard_map/ppermute | solution.py:128
  63.8 1.3 %collective-permute-done.other_ref = bf16[32,16,384]{2,1,0:T(8,128)(2,1)S(1)} collective-permute-done((bf16[32,16,384]{2,1,0:T(8,128)(2,1)S(1)}, bf16[32,16,384]{2,1,0:T(8,128)(2,1)S(1)}, u32[]{:S(2)}, u32[]{:S(2)}) %collective-permute-start) | collective-permute-done | bytes 393248 | tf_op jit(solution)/shard_map/ppermute | solution.py:128
  65.1 0.0 copy-done
  65.1 2.3 %third_kernel.1 = (bf16[32,16,256]{2,1,0:T(8,128)(2,1)S(1)}, f32[32,16,256]{2,1,0:T(8,128)S(1)}) custom-call(s32[1]{0:T(128)} %bitcast.at_ref, bf16[32,16,384]{2,1,0:T(8,128)(2,1)S(1)} %all_to_all.21.own_ref, bf16[32,16,384]{2,1,0:T(8,128)(2,1)S(1)} %collective-permute-done.other_ref, bf16[16,4,16,1024]{3,2,1,0:T(8,128)(2,1)S(1)} %bitcast.6), custom_call_target="tpu_custom_call" | custom-call | tf_op jit(solution)/shard_map/third_kernel/pallas_call | solution.py:112
  67.4 2.3 %collective-permute-start.1 = (bf16[32,16,256]{2,1,0:T(8,128)(2,1)S(1)}, bf16[32,16,256]{2,1,0:T(8,128)(2,1)S(1)}, u32[]{:S(2)}, u32[]{:S(2)}) collective-permute-start(bf16[32,16,256]{2,1,0:T(8,128)(2,1)S(1)} %get-tuple-element.8), channel_id=1, source_target_pairs={{0,1},{1,0},{2,3},{3,2},{4,5},{5,4},{6,7},{7,6},{8,9},{9,8},{10,11... | collective-permute-start | bytes 786440 | tf_op jit(solution)/shard_map/ppermute | solution.py:128
  69.7 1.1 %collective-permute-done.1.got_ref = bf16[32,16,256]{2,1,0:T(8,128)(2,1)S(1)} collective-permute-done((bf16[32,16,256]{2,1,0:T(8,128)(2,1)S(1)}, bf16[32,16,256]{2,1,0:T(8,128)(2,1)S(1)}, u32[]{:S(2)}, u32[]{:S(2)}) %collective-permute-start.1) | collective-permute-done | bytes 262176 | tf_op jit(solution)/shard_map/ppermute | solution.py:128
  70.9 15.8 %all_to_all.22.got_ref = bf16[32,16,256]{2,1,0:T(8,128)(2,1)S(1)} all-to-all(bf16[32,16,256]{2,1,0:T(8,128)(2,1)S(1)} %add_kernel.1), channel_id=1, replica_groups=mesh['xh'=2,'y'=8,'z'=16,'xl'=2,'c'=2] {'xh','y','xl'}, dimensions={0} | all-to-all | bytes 524288 | tf_op jit(solution)/shard_map/all_to_all | solution.py:124
  86.7 0.8 fourth_kernel.1
  87.6 18.1 %all_to_all.23.got_ref = f32[16,2,128]{2,1,0:T(2,128)S(1)} all-to-all(f32[16,2,128]{2,1,0:T(2,128)S(1)} %fourth_kernel.1), channel_id=1, replica_groups=mesh['xh'=2,'y'=8,'z'=16,'xl'=2,'c'=2] {'z'}, dimensions={0} | all-to-all | bytes 32768 | tf_op jit(solution)/shard_map/all_to_all | solution.py:124
  105.7 0.8 last_kernel.1
  (1 shorter events, 0.0 us)
Async XLA Ops:
  0.0 65.1 %copy-start = (bf16[1,1024,1024]{2,1,0:T(8,128)(2,1)S(1)}, bf16[1,1024,1024]{2,1,0:T(8,128)(2,1)}, u32[]{:S(2)}) copy-start(bf16[1,1024,1024]{2,1,0:T(8,128)(2,1)} %param.6) | copy-start | bytes 6291460
  56.1 9.0 %collective-permute-start = (bf16[32,16,384]{2,1,0:T(8,128)(2,1)S(1)}, bf16[32,16,384]{2,1,0:T(8,128)(2,1)S(1)}, u32[]{:S(2)}, u32[]{:S(2)}) collective-permute-start(bf16[32,16,384]{2,1,0:T(8,128)(2,1)S(1)} %all_to_all.21.own_ref), channel_id=1, source_target_pairs={{0,1},{1,0},{2,3},{3,2},{4,5},{5,4},{6,7},{7,6},{8,9},{9,8},{10,11... | collective-permute-start | bytes 1179656 | tf_op jit(solution)/shard_map/ppermute | solution.py:128
  67.4 3.4 %collective-permute-start.1 = (bf16[32,16,256]{2,1,0:T(8,128)(2,1)S(1)}, bf16[32,16,256]{2,1,0:T(8,128)(2,1)S(1)}, u32[]{:S(2)}, u32[]{:S(2)}) collective-permute-start(bf16[32,16,256]{2,1,0:T(8,128)(2,1)S(1)} %get-tuple-element.8), channel_id=1, source_target_pairs={{0,1},{1,0},{2,3},{3,2},{4,5},{5,4},{6,7},{7,6},{8,9},{9,8},{10,11... | collective-permute-start | bytes 786440 | tf_op jit(solution)/shard_map/ppermute | solution.py:128

commit v4 on v3

v4 whole, which is shorter than its diff:
```python
import jax
import jax.numpy as jnp
from jax import lax
from jax.experimental import pallas as pl
from jax.experimental.pallas import tpu as pltpu
from jax.sharding import Mesh, PartitionSpec as P

O = 256
V = 1024
W = 16
Z = 16
BLK = 16
XY = ("xh", "y", "xl")
ALL = ("xh", "y", "z", "xl", "c")
BF = jnp.bfloat16
F32 = jnp.float32


def iota(shape, axis):
    return lax.broadcasted_iota(jnp.int32, shape, axis)


def ones_at(mask, dtype=BF):
    return jnp.where(mask, 1.0, 0.0).astype(dtype)


def dot(a, b, ca, cb, precision=None):
    return lax.dot_general(
        a, b, (((ca,), (cb,)), ((), ())), precision=precision, preferred_element_type=F32
    )


def first_kernel(
    at_ref, pairs_hbm, screening_hbm, trials_hbm, out_ref, pairs_ref, screening_ref, trials_ref, columns_ref, sems
):
    copies = [pltpu.make_async_copy(pairs_hbm, pairs_ref, sems.at[0])]
    for k in range(4):
        part = pl.ds(256 * k, 256)
        copies.append(pltpu.make_async_copy(screening_hbm.at[:, part], screening_ref.at[:, part], sems.at[1 + k]))
    copies.append(pltpu.make_async_copy(trials_hbm, trials_ref, sems.at[5]))
    for copy in copies:
        copy.start()
    copies[0].wait()
    for k in range(4):
        copies[1 + k].wait()
        part = slice(256 * k, 256 * (k + 1))
        columns_ref[part, :] = dot(pairs_ref[...], screening_ref[:, part], 1, 0).T
    copies[5].wait()
    mine = iota((BLK, O), 0) == at_ref[0]
    row = jnp.sum(jnp.where(mine, trials_ref[...].astype(F32), 0.0), 0, keepdims=True)
    rank = iota((8, 128), 0)
    tail = jnp.where(rank == 0, row[:, :128], jnp.where(rank == 1, row[:, 128:], 0.0)).astype(BF)
    for z in range(Z):
        for x in range(2):
            left, right = (columns_ref[pl.ds(4 * z + 2 * x + c, W, 64), :] for c in range(2))
            out_ref[z, W * x : W * (x + 1), :] = jnp.concatenate([left, right], 1).astype(BF)
        out_ref[z, 32:, :] = tail


def second_kernel(got_ref, out_ref, rows_ref):
    rows_ref[...] = got_ref[...].reshape(Z * 40, 128).astype(F32)
    trials = jnp.concatenate([rows_ref[pl.ds(r, Z, 40), :] for r in (32, 33)], 1).astype(BF)
    for w in range(W):
        for x in range(2):
            out_ref[2 * w + x, :, :128] = rows_ref[pl.ds(W * x + w, Z, 40), :].astype(BF)
            out_ref[2 * w + x, :, 128:] = trials


def ordered(ref):
    flip = ones_at(iota((O, O), 1) == iota((O, O), 0) % W * Z + iota((O, O), 0) // W)
    tiles = [jnp.concatenate([ref[2 * w + x, :, 128:] for w in range(W)], 0) for x in range(2)]
    return [dot(flip, tile, 1, 0).astype(BF) for tile in tiles]


def own_kernel(own_ref, trials_ref):
    trials_ref[0], trials_ref[1] = ordered(own_ref)


def partial(of, screened_ref, trials_ref, virtual_ref, out_ref):
    for x in range(2):
        rows = virtual_ref[:, 2 * x + of].reshape(O, V)
        halves = dot(rows, trials_ref[...], 1, 0).astype(BF)
        part = dot(screened_ref[...], halves, 1, 1).astype(out_ref.dtype)
        for w in range(W):
            out_ref[2 * w + x] = part[BLK * w : BLK * (w + 1), :]


def send_kernel(at_ref, own_ref, own_trials_ref, other_ref, virtual_ref, send_ref, screened_ref, trials_ref):
    core = at_ref[0]
    here = iota((BLK, 128), 1) // 64 == core
    for w in range(W):
        for x in range(2):
            moved = pltpu.roll(other_ref[2 * w + x, :, :128].astype(F32), 64, 1)
            tile = jnp.where(here, own_ref[2 * w + x, :, :128].astype(F32), moved)
            screened_ref[BLK * w : BLK * (w + 1), 128 * x : 128 * (x + 1)] = tile.astype(BF)
    for tiles, c in (((own_trials_ref[0], own_trials_ref[1]), core), (ordered(other_ref), 1 - core)):
        for x in range(2):
            for z in range(Z):
                start = pl.multiple_of(64 * z + 32 * x + BLK * c, BLK)
                trials_ref[pl.ds(start, BLK), :] = tiles[x][W * z : W * (z + 1), :]
    partial(1 - core, screened_ref, trials_ref, virtual_ref, send_ref)


def keep_kernel(at_ref, screened_ref, trials_ref, virtual_ref, keep_ref):
    partial(at_ref[0], screened_ref, trials_ref, virtual_ref, keep_ref)


def add_kernel(kept_ref, got_ref, out_ref):
    out_ref[...] = (kept_ref[...] + got_ref[...].astype(F32)).astype(BF)


def fourth_kernel(got_ref, out_ref):
    total = jnp.sum(got_ref[...].astype(F32), 0)
    row, chunk = iota((8, 128), 0), iota((8, 128), 1) // BLK
    for r in range(2):
        for h in range(2):
            t = total[8 * r : 8 * (r + 1), 128 * h : 128 * (h + 1)]
            for s in (1, 2, 4):
                up = pltpu.roll(pltpu.roll(t, 8 - s, 0), BLK * s, 1)
                down = pltpu.roll(pltpu.roll(t, s, 0), 128 - BLK * s, 1)
                high, right = row & s != 0, chunk & s != 0
                t = jnp.where(high == right, t, jnp.where(right, up, down))
            out_ref[8 * h : 8 * (h + 1), r, :] = t


def last_kernel(got_ref, out_ref):
    rows = []
    for r in range(2):
        total = jnp.sum(got_ref[:, r, :], 0, keepdims=True)
        t = jnp.where(iota((8, 128), 0) == iota((8, 128), 1) // BLK, total, 0.0)
        for s in (64, 32, BLK):
            t = t + pltpu.roll(t, s, 1)
        rows.append(t)
    out_ref[...] = jnp.concatenate(rows, 0).T[:BLK, :].reshape(BLK, 1, BLK)


def in_vmem(v):
    return pltpu.with_memory_space_constraint(v, pltpu.VMEM)


def in_hbm(v):
    return pltpu.with_memory_space_constraint(v, pltpu.HBM)


def vmem_out(shape, dtype):
    return pltpu.VMEM(shape, dtype)


def call(body, outs, *args, scratch=(), limit=24 << 20, hbm=False):
    vmem = pl.BlockSpec(memory_space=pltpu.VMEM)
    space = pl.BlockSpec(memory_space=pltpu.HBM) if hbm else vmem
    specs = [pl.BlockSpec(memory_space=pltpu.SMEM) if a.dtype == jnp.int32 else space for a in args]
    return pl.pallas_call(
        body,
        out_shape=outs,
        in_specs=specs,
        out_specs=jax.tree.map(lambda o: vmem, outs),
        scratch_shapes=scratch,
        compiler_params=pltpu.CompilerParams(vmem_limit_bytes=limit),
        name=body.__name__,
    )(*args)


def swap(v, axis):
    return in_vmem(lax.all_to_all(v, axis, 0, 0, tiled=True))


def across(v):
    return in_vmem(lax.ppermute(v, "c", [(0, 1), (1, 0)]))


def per_device(pair_integrals, screening, virtual_integrals, trials):
    at = lax.axis_index(("xh", "y")).reshape(1).astype(jnp.int32)
    core = lax.axis_index("c").reshape(1).astype(jnp.int32)
    sent = call(
        first_kernel,
        vmem_out((Z, 40, 128), BF),
        at,
        in_hbm(pair_integrals),
        in_hbm(screening),
        in_hbm(trials.reshape(O, BLK).T),
        scratch=[
            pltpu.VMEM((64, V), BF),
            pltpu.VMEM((V, V), BF),
            pltpu.VMEM((BLK, O), BF),
            pltpu.VMEM((V, 64), F32),
            pltpu.SemaphoreType.DMA((6,)),
        ],
        hbm=True,
    )
    got = swap(sent, "z")
    sent = call(second_kernel, vmem_out((2 * W, Z, 384), BF), got, scratch=[pltpu.VMEM((Z * 40, 128), F32)])
    own = swap(sent, XY)
    other = across(own)
    own_trials = call(own_kernel, vmem_out((2, O, O), BF), own)
    virtual = in_vmem(virtual_integrals.reshape(Z, 4, BLK, V))
    sent, screened, whole = call(
        send_kernel,
        (vmem_out((2 * W, BLK, O), BF), vmem_out((O, O), BF), vmem_out((V, O), BF)),
        core,
        own,
        own_trials,
        other,
        virtual,
    )
    got = across(sent)
    kept = call(keep_kernel, vmem_out((2 * W, BLK, O), F32), core, screened, whole, virtual)
    got = swap(call(add_kernel, vmem_out((2 * W, BLK, O), BF), kept, got), XY)
    got = swap(call(fourth_kernel, vmem_out((Z, 2, 128), F32), got), "z")
    return call(last_kernel, jax.ShapeDtypeStruct((BLK, 1, BLK), F32), got)


def solution(mesh):
    chips = Mesh(mesh.devices.reshape(2, 8, 16, 2, 2), ALL)
    return jax.shard_map(
        per_device,
        mesh=chips,
        in_specs=(
            P(ALL, None),
            P(),
            P(ALL, None, None),
            P(None, None, ("z", "xl", "c")),
        ),
        out_specs=P(("z", "xl", "c"), None, ("xh", "y")),
        check_vma=False,
    )
```

time: 108 us -> 107 us (level)
  waiting for transfers between devices: 2.46 us -> 1.17 us
    ppermute x2, waiting for transfers between devices: 2.46 us -> 1.17 us  [across(): return in_vmem(lax.ppermute(v, 'c', [(0, 1), (1, 0)]))]
    pallas_call x6 -> x8, Pallas kernels: 6.65 us -> 6.93 us  [call(): pl.pallas_call(body, out_shape=outs, in_specs=specs, out_specs=jax.tree.m...]
  transfers between devices with their start and end apart: 2 -> 2, of which waited for: 2 -> 2; matrix products, arithmetic and copies ran while one was open for 0% -> 0% of each run, Pallas kernels for 0% -> 1%
where the time goes in v4:
time: 107 us; the launch traced here: 105 us
  blocking collectives  87.4 us (82%)
  starting transfers between devices  9.94 us (9%)
  Pallas kernels  6.93 us (6%)
  waiting for transfers between devices  1.17 us (1%)
    all_to_all x4, blocking collectives, swap(): return in_vmem(lax.all_to_all(v, axis, 0, 0, tiled=True))  87.4 us
    ppermute x2, starting transfers between devices, across(): return in_vmem(lax.ppermute(v, 'c', [(0, 1), (1, 0)]))  9.94 us
    pallas_call x8, Pallas kernels, call(): pl.pallas_call(body, out_shape=outs, in_specs=specs, out_specs=jax.tree.m...  6.93 us
  transfers between devices with their start and end apart: 2, of which 2 were waited for; matrix products, arithmetic and copies ran while one was open for 0% of the time, Pallas kernels for 1%

profile of v4, /device:TPU:1, one launch (start us, length us, event | category | flops | bytes accessed | tf_op | source)
XLA Modules:
  0.0 105.5 jit_solution(2199227587505913697)
XLA Ops:
  0.0 0.0 copy-start
  0.0 3.0 %first_kernel.1 = bf16[16,40,128]{2,1,0:T(8,128)(2,1)S(1)} custom-call(s32[1]{0:T(128)} %bitcast.1.at_ref, bf16[64,1024]{1,0:T(8,128)(2,1)} %pairs_hbm.1, bf16[1024,1024]{1,0:T(8,128)(2,1)} %screening_hbm.1, bf16[16,256]{1,0:T(8,128)(2,1)} %bitcast.8), custom_call_target="tpu_custom_call" | custom-call | tf_op jit(solution)/shard_map/first_kernel/pallas_call | solution.py:153
  3.1 31.4 %all_to_all.20.got_ref = bf16[16,40,128]{2,1,0:T(8,128)(2,1)S(1)} all-to-all(bf16[16,40,128]{2,1,0:T(8,128)(2,1)S(1)} %first_kernel.1), channel_id=1, replica_groups=mesh['xh'=2,'y'=8,'z'=16,'xl'=2,'c'=2] {'z'}, dimensions={0} | all-to-all | bytes 327680 | tf_op jit(solution)/shard_map/all_to_all | solution.py:165
  34.4 0.1 second_kernel.1
  34.5 22.1 %all_to_all.21.own_ref = bf16[32,16,384]{2,1,0:T(8,128)(2,1)S(1)} all-to-all(bf16[32,16,384]{2,1,0:T(8,128)(2,1)S(1)} %second_kernel.1), channel_id=1, replica_groups=mesh['xh'=2,'y'=8,'z'=16,'xl'=2,'c'=2] {'xh','y','xl'}, dimensions={0} | all-to-all | bytes 786432 | tf_op jit(solution)/shard_map/all_to_all | solution.py:165
  56.6 7.7 %collective-permute-start = (bf16[32,16,384]{2,1,0:T(8,128)(2,1)S(1)}, bf16[32,16,384]{2,1,0:T(8,128)(2,1)S(1)}, u32[]{:S(2)}, u32[]{:S(2)}) collective-permute-start(bf16[32,16,384]{2,1,0:T(8,128)(2,1)S(1)} %all_to_all.21.own_ref), channel_id=1, source_target_pairs={{0,1},{1,0},{2,3},{3,2},{4,5},{5,4},{6,7},{7,6},{8,9},{9,8},{10,11... | collective-permute-start | bytes 1179656 | tf_op jit(solution)/shard_map/ppermute | solution.py:169
  64.2 0.2 own_kernel.1.own_trials_ref
  64.5 1.1 %collective-permute-done.other_ref = bf16[32,16,384]{2,1,0:T(8,128)(2,1)S(1)} collective-permute-done((bf16[32,16,384]{2,1,0:T(8,128)(2,1)S(1)}, bf16[32,16,384]{2,1,0:T(8,128)(2,1)S(1)}, u32[]{:S(2)}, u32[]{:S(2)}) %collective-permute-start) | collective-permute-done | bytes 393248 | tf_op jit(solution)/shard_map/ppermute | solution.py:169
  65.6 0.0 copy-done
  65.6 1.3 %send_kernel.1 = (bf16[32,16,256]{2,1,0:T(8,128)(2,1)S(1)}, bf16[256,256]{1,0:T(8,128)(2,1)S(1)}, bf16[1024,256]{1,0:T(8,128)(2,1)S(1)}) custom-call(s32[1]{0:T(128)} %bitcast.at_ref, bf16[32,16,384]{2,1,0:T(8,128)(2,1)S(1)} %all_to_all.21.own_ref, bf16[2,256,256]{2,1,0:T(8,128)(2,1)S(1)} %own_kernel.1.own_trials_ref, ...), custom_call_target="tpu_custom_call" | custom-call | tf_op jit(solution)/shard_map/send_kernel/pallas_call | solution.py:153
  66.9 2.3 %collective-permute-start.1 = (bf16[32,16,256]{2,1,0:T(8,128)(2,1)S(1)}, bf16[32,16,256]{2,1,0:T(8,128)(2,1)S(1)}, u32[]{:S(2)}, u32[]{:S(2)}) collective-permute-start(bf16[32,16,256]{2,1,0:T(8,128)(2,1)S(1)} %get-tuple-element.10), channel_id=1, source_target_pairs={{0,1},{1,0},{2,3},{3,2},{4,5},{5,4},{6,7},{7,6},{8,9},{9,8},{10,11... | collective-permute-start | bytes 786440 | tf_op jit(solution)/shard_map/ppermute | solution.py:169
  69.2 1.1 %keep_kernel.1.kept_ref = f32[32,16,256]{2,1,0:T(8,128)S(1)} custom-call(s32[1]{0:T(128)} %bitcast.at_ref, bf16[256,256]{1,0:T(8,128)(2,1)S(1)} %get-tuple-element.8.screened_ref, bf16[1024,256]{1,0:T(8,128)(2,1)S(1)} %get-tuple-element.9.trials_ref, bf16[16,4,16,1024]{3,2,1,0:T(8,128)(2,1)S(1)} %bitcast.7), custom_call_target="tpu_custom_call" | custom-call | tf_op jit(solution)/shard_map/keep_kernel/pallas_call | solution.py:153
  70.2 0.1 collective-permute-done.1.got_ref
  70.4 15.8 %all_to_all.22.got_ref = bf16[32,16,256]{2,1,0:T(8,128)(2,1)S(1)} all-to-all(bf16[32,16,256]{2,1,0:T(8,128)(2,1)S(1)} %add_kernel.1), channel_id=1, replica_groups=mesh['xh'=2,'y'=8,'z'=16,'xl'=2,'c'=2] {'xh','y','xl'}, dimensions={0} | all-to-all | bytes 524288 | tf_op jit(solution)/shard_map/all_to_all | solution.py:165
  86.2 0.3 fourth_kernel.1
  86.5 18.1 %all_to_all.23.got_ref = f32[16,2,128]{2,1,0:T(2,128)S(1)} all-to-all(f32[16,2,128]{2,1,0:T(2,128)S(1)} %fourth_kernel.1), channel_id=1, replica_groups=mesh['xh'=2,'y'=8,'z'=16,'xl'=2,'c'=2] {'z'}, dimensions={0} | all-to-all | bytes 32768 | tf_op jit(solution)/shard_map/all_to_all | solution.py:165
  104.6 0.9 last_kernel.1
  (1 shorter events, 0.0 us)
Async XLA Ops:
  0.0 65.6 %copy-start = (bf16[1,1024,1024]{2,1,0:T(8,128)(2,1)S(1)}, bf16[1,1024,1024]{2,1,0:T(8,128)(2,1)}, u32[]{:S(2)}) copy-start(bf16[1,1024,1024]{2,1,0:T(8,128)(2,1)} %param.6) | copy-start | bytes 6291460
  56.6 9.0 %collective-permute-start = (bf16[32,16,384]{2,1,0:T(8,128)(2,1)S(1)}, bf16[32,16,384]{2,1,0:T(8,128)(2,1)S(1)}, u32[]{:S(2)}, u32[]{:S(2)}) collective-permute-start(bf16[32,16,384]{2,1,0:T(8,128)(2,1)S(1)} %all_to_all.21.own_ref), channel_id=1, source_target_pairs={{0,1},{1,0},{2,3},{3,2},{4,5},{5,4},{6,7},{7,6},{8,9},{9,8},{10,11... | collective-permute-start | bytes 1179656 | tf_op jit(solution)/shard_map/ppermute | solution.py:169
  66.9 3.4 %collective-permute-start.1 = (bf16[32,16,256]{2,1,0:T(8,128)(2,1)S(1)}, bf16[32,16,256]{2,1,0:T(8,128)(2,1)S(1)}, u32[]{:S(2)}, u32[]{:S(2)}) collective-permute-start(bf16[32,16,256]{2,1,0:T(8,128)(2,1)S(1)} %get-tuple-element.10), channel_id=1, source_target_pairs={{0,1},{1,0},{2,3},{3,2},{4,5},{5,4},{6,7},{7,6},{8,9},{9,8},{10,11... | collective-permute-start | bytes 786440 | tf_op jit(solution)/shard_map/ppermute | solution.py:169

commit v5 on v4

--- a/solution.py
+++ b/solution.py
@@ -10,6 +10,7 @@
 W = 16
 Z = 16
 BLK = 16
+STEP = 72
 XY = ("xh", "y", "xl")
 ALL = ("xh", "y", "z", "xl", "c")
 BF = jnp.bfloat16
@@ -34,25 +35,26 @@
     at_ref, pairs_hbm, screening_hbm, trials_hbm, out_ref, pairs_ref, screening_ref, trials_ref, columns_ref, sems
 ):
     copies = [pltpu.make_async_copy(pairs_hbm, pairs_ref, sems.at[0])]
-    for k in range(4):
-        part = pl.ds(256 * k, 256)
+    for k in range(2):
+        part = pl.ds(O * 2 * k, O * 2)
         copies.append(pltpu.make_async_copy(screening_hbm.at[:, part], screening_ref.at[:, part], sems.at[1 + k]))
-    copies.append(pltpu.make_async_copy(trials_hbm, trials_ref, sems.at[5]))
+    copies.append(pltpu.make_async_copy(trials_hbm, trials_ref, sems.at[3]))
     for copy in copies:
         copy.start()
     copies[0].wait()
-    for k in range(4):
+    for k in range(2):
         copies[1 + k].wait()
-        part = slice(256 * k, 256 * (k + 1))
-        columns_ref[part, :] = dot(pairs_ref[...], screening_ref[:, part], 1, 0).T
-    copies[5].wait()
+        columns = dot(pairs_ref[...], screening_ref[:, O * 2 * k : O * 2 * (k + 1)], 1, 0).T
+        for w in range(8):
+            columns_ref[pl.ds(STEP * (8 * k + w), 64), :] = columns[64 * w : 64 * (w + 1), :]
+    copies[3].wait()
     mine = iota((BLK, O), 0) == at_ref[0]
     row = jnp.sum(jnp.where(mine, trials_ref[...].astype(F32), 0.0), 0, keepdims=True)
     rank = iota((8, 128), 0)
     tail = jnp.where(rank == 0, row[:, :128], jnp.where(rank == 1, row[:, 128:], 0.0)).astype(BF)
     for z in range(Z):
         for x in range(2):
-            left, right = (columns_ref[pl.ds(4 * z + 2 * x + c, W, 64), :] for c in range(2))
+            left, right = (columns_ref[pl.ds(4 * z + 2 * x + c, W, STEP), :] for c in range(2))
             out_ref[z, W * x : W * (x + 1), :] = jnp.concatenate([left, right], 1).astype(BF)
         out_ref[z, 32:, :] = tail
 
@@ -183,8 +185,8 @@
             pltpu.VMEM((64, V), BF),
             pltpu.VMEM((V, V), BF),
             pltpu.VMEM((BLK, O), BF),
-            pltpu.VMEM((V, 64), F32),
-            pltpu.SemaphoreType.DMA((6,)),
+            pltpu.VMEM((W * STEP, 64), F32),
+            pltpu.SemaphoreType.DMA((4,)),
         ],
         hbm=True,
     )

time: 107 us -> 106 us (level)
  no operation moved by 1% of the time
where the time goes in v5:
time: 106 us; the launch traced here: 105 us
  blocking collectives  87.4 us (82%)
  starting transfers between devices  9.94 us (9%)
  Pallas kernels  6.3 us (6%)
  waiting for transfers between devices  1.17 us (1%)
    all_to_all x4, blocking collectives, swap(): return in_vmem(lax.all_to_all(v, axis, 0, 0, tiled=True))  87.4 us
    ppermute x2, starting transfers between devices, across(): return in_vmem(lax.ppermute(v, 'c', [(0, 1), (1, 0)]))  9.94 us
    pallas_call x8, Pallas kernels, call(): pl.pallas_call(body, out_shape=outs, in_specs=specs, out_specs=jax.tree.m...  6.3 us
  transfers between devices with their start and end apart: 2, of which 2 were waited for; matrix products, arithmetic and copies ran while one was open for 0% of the time, Pallas kernels for 1%

profile of v5, /device:TPU:1, one launch (start us, length us, event | category | flops | bytes accessed | tf_op | source)
XLA Modules:
  0.0 104.8 jit_solution(14876511866038618321)
XLA Ops:
  0.0 0.0 copy-start
  0.0 2.4 %first_kernel.1 = bf16[16,40,128]{2,1,0:T(8,128)(2,1)S(1)} custom-call(s32[1]{0:T(128)} %bitcast.1.at_ref, bf16[64,1024]{1,0:T(8,128)(2,1)} %pairs_hbm.1, bf16[1024,1024]{1,0:T(8,128)(2,1)} %screening_hbm.1, bf16[16,256]{1,0:T(8,128)(2,1)} %bitcast.8), custom_call_target="tpu_custom_call" | custom-call | tf_op jit(solution)/shard_map/first_kernel/pallas_call | solution.py:155
  2.4 31.4 %all_to_all.20.got_ref = bf16[16,40,128]{2,1,0:T(8,128)(2,1)S(1)} all-to-all(bf16[16,40,128]{2,1,0:T(8,128)(2,1)S(1)} %first_kernel.1), channel_id=1, replica_groups=mesh['xh'=2,'y'=8,'z'=16,'xl'=2,'c'=2] {'z'}, dimensions={0} | all-to-all | bytes 327680 | tf_op jit(solution)/shard_map/all_to_all | solution.py:167
  33.8 0.1 second_kernel.1
  33.9 22.1 %all_to_all.21.own_ref = bf16[32,16,384]{2,1,0:T(8,128)(2,1)S(1)} all-to-all(bf16[32,16,384]{2,1,0:T(8,128)(2,1)S(1)} %second_kernel.1), channel_id=1, replica_groups=mesh['xh'=2,'y'=8,'z'=16,'xl'=2,'c'=2] {'xh','y','xl'}, dimensions={0} | all-to-all | bytes 786432 | tf_op jit(solution)/shard_map/all_to_all | solution.py:167
  55.9 7.7 %collective-permute-start = (bf16[32,16,384]{2,1,0:T(8,128)(2,1)S(1)}, bf16[32,16,384]{2,1,0:T(8,128)(2,1)S(1)}, u32[]{:S(2)}, u32[]{:S(2)}) collective-permute-start(bf16[32,16,384]{2,1,0:T(8,128)(2,1)S(1)} %all_to_all.21.own_ref), channel_id=1, source_target_pairs={{0,1},{1,0},{2,3},{3,2},{4,5},{5,4},{6,7},{7,6},{8,9},{9,8},{10,11... | collective-permute-start | bytes 1179656 | tf_op jit(solution)/shard_map/ppermute | solution.py:171
  63.6 0.2 own_kernel.1.own_trials_ref
  63.8 1.1 %collective-permute-done.other_ref = bf16[32,16,384]{2,1,0:T(8,128)(2,1)S(1)} collective-permute-done((bf16[32,16,384]{2,1,0:T(8,128)(2,1)S(1)}, bf16[32,16,384]{2,1,0:T(8,128)(2,1)S(1)}, u32[]{:S(2)}, u32[]{:S(2)}) %collective-permute-start) | collective-permute-done | bytes 393248 | tf_op jit(solution)/shard_map/ppermute | solution.py:171
  64.9 0.0 copy-done
  64.9 1.3 %send_kernel.1 = (bf16[32,16,256]{2,1,0:T(8,128)(2,1)S(1)}, bf16[256,256]{1,0:T(8,128)(2,1)S(1)}, bf16[1024,256]{1,0:T(8,128)(2,1)S(1)}) custom-call(s32[1]{0:T(128)} %bitcast.at_ref, bf16[32,16,384]{2,1,0:T(8,128)(2,1)S(1)} %all_to_all.21.own_ref, bf16[2,256,256]{2,1,0:T(8,128)(2,1)S(1)} %own_kernel.1.own_trials_ref, ...), custom_call_target="tpu_custom_call" | custom-call | tf_op jit(solution)/shard_map/send_kernel/pallas_call | solution.py:155
  66.2 2.3 %collective-permute-start.1 = (bf16[32,16,256]{2,1,0:T(8,128)(2,1)S(1)}, bf16[32,16,256]{2,1,0:T(8,128)(2,1)S(1)}, u32[]{:S(2)}, u32[]{:S(2)}) collective-permute-start(bf16[32,16,256]{2,1,0:T(8,128)(2,1)S(1)} %get-tuple-element.10), channel_id=1, source_target_pairs={{0,1},{1,0},{2,3},{3,2},{4,5},{5,4},{6,7},{7,6},{8,9},{9,8},{10,11... | collective-permute-start | bytes 786440 | tf_op jit(solution)/shard_map/ppermute | solution.py:171
  68.5 1.1 %keep_kernel.1.kept_ref = f32[32,16,256]{2,1,0:T(8,128)S(1)} custom-call(s32[1]{0:T(128)} %bitcast.at_ref, bf16[256,256]{1,0:T(8,128)(2,1)S(1)} %get-tuple-element.8.screened_ref, bf16[1024,256]{1,0:T(8,128)(2,1)S(1)} %get-tuple-element.9.trials_ref, bf16[16,4,16,1024]{3,2,1,0:T(8,128)(2,1)S(1)} %bitcast.7), custom_call_target="tpu_custom_call" | custom-call | tf_op jit(solution)/shard_map/keep_kernel/pallas_call | solution.py:155
  69.6 0.1 collective-permute-done.1.got_ref
  69.7 15.8 %all_to_all.22.got_ref = bf16[32,16,256]{2,1,0:T(8,128)(2,1)S(1)} all-to-all(bf16[32,16,256]{2,1,0:T(8,128)(2,1)S(1)} %add_kernel.1), channel_id=1, replica_groups=mesh['xh'=2,'y'=8,'z'=16,'xl'=2,'c'=2] {'xh','y','xl'}, dimensions={0} | all-to-all | bytes 524288 | tf_op jit(solution)/shard_map/all_to_all | solution.py:167
  85.6 0.3 fourth_kernel.1
  85.8 18.1 %all_to_all.23.got_ref = f32[16,2,128]{2,1,0:T(2,128)S(1)} all-to-all(f32[16,2,128]{2,1,0:T(2,128)S(1)} %fourth_kernel.1), channel_id=1, replica_groups=mesh['xh'=2,'y'=8,'z'=16,'xl'=2,'c'=2] {'z'}, dimensions={0} | all-to-all | bytes 32768 | tf_op jit(solution)/shard_map/all_to_all | solution.py:167
  103.9 0.9 last_kernel.1
  (1 shorter events, 0.0 us)
Async XLA Ops:
  0.0 64.9 %copy-start = (bf16[1,1024,1024]{2,1,0:T(8,128)(2,1)S(1)}, bf16[1,1024,1024]{2,1,0:T(8,128)(2,1)}, u32[]{:S(2)}) copy-start(bf16[1,1024,1024]{2,1,0:T(8,128)(2,1)} %param.6) | copy-start | bytes 6291460
  55.9 9.0 %collective-permute-start = (bf16[32,16,384]{2,1,0:T(8,128)(2,1)S(1)}, bf16[32,16,384]{2,1,0:T(8,128)(2,1)S(1)}, u32[]{:S(2)}, u32[]{:S(2)}) collective-permute-start(bf16[32,16,384]{2,1,0:T(8,128)(2,1)S(1)} %all_to_all.21.own_ref), channel_id=1, source_target_pairs={{0,1},{1,0},{2,3},{3,2},{4,5},{5,4},{6,7},{7,6},{8,9},{9,8},{10,11... | collective-permute-start | bytes 1179656 | tf_op jit(solution)/shard_map/ppermute | solution.py:171
  66.2 3.4 %collective-permute-start.1 = (bf16[32,16,256]{2,1,0:T(8,128)(2,1)S(1)}, bf16[32,16,256]{2,1,0:T(8,128)(2,1)S(1)}, u32[]{:S(2)}, u32[]{:S(2)}) collective-permute-start(bf16[32,16,256]{2,1,0:T(8,128)(2,1)S(1)} %get-tuple-element.10), channel_id=1, source_target_pairs={{0,1},{1,0},{2,3},{3,2},{4,5},{5,4},{6,7},{7,6},{8,9},{9,8},{10,11... | collective-permute-start | bytes 786440 | tf_op jit(solution)/shard_map/ppermute | solution.py:171

commit v6 on v5

--- a/solution.py
+++ b/solution.py
@@ -50,21 +50,20 @@
     copies[3].wait()
     mine = iota((BLK, O), 0) == at_ref[0]
     row = jnp.sum(jnp.where(mine, trials_ref[...].astype(F32), 0.0), 0, keepdims=True)
-    rank = iota((8, 128), 0)
-    tail = jnp.where(rank == 0, row[:, :128], jnp.where(rank == 1, row[:, 128:], 0.0)).astype(BF)
+    tail = jnp.where(iota((2, 128), 0) == 0, row[:, :128], row[:, 128:]).astype(BF)
     for z in range(Z):
         for x in range(2):
             left, right = (columns_ref[pl.ds(4 * z + 2 * x + c, W, STEP), :] for c in range(2))
-            out_ref[z, W * x : W * (x + 1), :] = jnp.concatenate([left, right], 1).astype(BF)
-        out_ref[z, 32:, :] = tail
+            out_ref[z, 8 * x : 8 * (x + 1)] = jnp.concatenate([left, right], 1).astype(BF).reshape(8, 2, 128)
+        out_ref[z, 16] = tail
 
 
 def second_kernel(got_ref, out_ref, rows_ref):
-    rows_ref[...] = got_ref[...].reshape(Z * 40, 128).astype(F32)
-    trials = jnp.concatenate([rows_ref[pl.ds(r, Z, 40), :] for r in (32, 33)], 1).astype(BF)
+    rows_ref[...] = got_ref[...].reshape(Z * 34, 128).astype(F32)
+    trials = jnp.concatenate([rows_ref[pl.ds(r, Z, 34), :] for r in (32, 33)], 1).astype(BF)
     for w in range(W):
         for x in range(2):
-            out_ref[2 * w + x, :, :128] = rows_ref[pl.ds(W * x + w, Z, 40), :].astype(BF)
+            out_ref[2 * w + x, :, :128] = rows_ref[pl.ds(W * x + w, Z, 34), :].astype(BF)
             out_ref[2 * w + x, :, 128:] = trials
 
 
@@ -74,8 +73,11 @@
     return [dot(flip, tile, 1, 0).astype(BF) for tile in tiles]
 
 
-def own_kernel(own_ref, trials_ref):
+def own_kernel(own_ref, virtual_hbm, trials_ref, virtual_ref, sem):
+    copy = pltpu.make_async_copy(virtual_hbm, virtual_ref, sem)
+    copy.start()
     trials_ref[0], trials_ref[1] = ordered(own_ref)
+    copy.wait()
 
 
 def partial(of, screened_ref, trials_ref, virtual_ref, out_ref):
@@ -148,10 +150,11 @@
     return pltpu.VMEM(shape, dtype)
 
 
-def call(body, outs, *args, scratch=(), limit=24 << 20, hbm=False):
+def call(body, outs, *args, scratch=(), limit=24 << 20, hbm=()):
     vmem = pl.BlockSpec(memory_space=pltpu.VMEM)
-    space = pl.BlockSpec(memory_space=pltpu.HBM) if hbm else vmem
-    specs = [pl.BlockSpec(memory_space=pltpu.SMEM) if a.dtype == jnp.int32 else space for a in args]
+    specs = [pl.BlockSpec(memory_space=pltpu.SMEM) if a.dtype == jnp.int32 else vmem for a in args]
+    for at in hbm:
+        specs[at] = pl.BlockSpec(memory_space=pltpu.HBM)
     return pl.pallas_call(
         body,
         out_shape=outs,
@@ -176,7 +179,7 @@
     core = lax.axis_index("c").reshape(1).astype(jnp.int32)
     sent = call(
         first_kernel,
-        vmem_out((Z, 40, 128), BF),
+        vmem_out((Z, 17, 2, 128), BF),
         at,
         in_hbm(pair_integrals),
         in_hbm(screening),
@@ -188,14 +191,20 @@
             pltpu.VMEM((W * STEP, 64), F32),
             pltpu.SemaphoreType.DMA((4,)),
         ],
-        hbm=True,
+        hbm=(1, 2, 3),
     )
     got = swap(sent, "z")
-    sent = call(second_kernel, vmem_out((2 * W, Z, 384), BF), got, scratch=[pltpu.VMEM((Z * 40, 128), F32)])
+    sent = call(second_kernel, vmem_out((2 * W, Z, 384), BF), got, scratch=[pltpu.VMEM((Z * 34, 128), F32)])
     own = swap(sent, XY)
     other = across(own)
-    own_trials = call(own_kernel, vmem_out((2, O, O), BF), own)
-    virtual = in_vmem(virtual_integrals.reshape(Z, 4, BLK, V))
+    own_trials, virtual = call(
+        own_kernel,
+        (vmem_out((2, O, O), BF), vmem_out((Z, 4, BLK, V), BF)),
+        own,
+        in_hbm(virtual_integrals.reshape(Z, 4, BLK, V)),
+        scratch=[pltpu.SemaphoreType.DMA(())],
+        hbm=(1,),
+    )
     sent, screened, whole = call(
         send_kernel,
         (vmem_out((2 * W, BLK, O), BF), vmem_out((O, O), BF), vmem_out((V, O), BF)),

time: 106 us -> 105 us (level)
  Pallas kernels: 6.3 us -> 7.69 us
    pallas_call x8, Pallas kernels: 6.3 us -> 7.69 us  [call(): pl.pallas_call(body, out_shape=outs, in_specs=specs, out_specs=jax.tree.m...]
  transfers between devices with their start and end apart: 2 -> 2, of which waited for: 2 -> 1; matrix products, arithmetic and copies ran while one was open for 0% -> 0% of each run, Pallas kernels for 1% -> 3%
where the time goes in v6:
time: 105 us; the launch traced here: 104 us
  blocking collectives  86.7 us (83%)
  starting transfers between devices  9.05 us (9%)
  Pallas kernels  7.69 us (7%)
    all_to_all x4, blocking collectives, swap(): return in_vmem(lax.all_to_all(v, axis, 0, 0, tiled=True))  86.7 us
    ppermute x2, starting transfers between devices, across(): return in_vmem(lax.ppermute(v, 'c', [(0, 1), (1, 0)]))  9.05 us
    pallas_call x8, Pallas kernels, call(): pl.pallas_call(body, out_shape=outs, in_specs=specs, out_specs=jax.tree.m...  7.69 us
  transfers between devices with their start and end apart: 2, of which 1 were waited for; matrix products, arithmetic and copies ran while one was open for 0% of the time, Pallas kernels for 3%

profile of v6, /device:TPU:1, one launch (start us, length us, event | category | flops | bytes accessed | tf_op | source)
XLA Modules:
  0.0 103.9 jit_solution(3693871491532677082)
XLA Ops:
  0.0 2.3 %first_kernel.1 = bf16[16,17,2,128]{3,2,1,0:T(2,128)(2,1)S(1)} custom-call(s32[1]{0:T(128)} %bitcast.1.at_ref, bf16[64,1024]{1,0:T(8,128)(2,1)} %pairs_hbm.1, bf16[1024,1024]{1,0:T(8,128)(2,1)} %screening_hbm.1, bf16[16,256]{1,0:T(8,128)(2,1)} %bitcast.7), custom_call_target="tpu_custom_call" | custom-call | tf_op jit(solution)/shard_map/first_kernel/pallas_call | solution.py:158
  2.4 31.2 %all_to_all.20.got_ref = bf16[16,17,2,128]{3,2,1,0:T(2,128)(2,1)S(1)} all-to-all(bf16[16,17,2,128]{3,2,1,0:T(2,128)(2,1)S(1)} %first_kernel.1), channel_id=1, replica_groups=mesh['xh'=2,'y'=8,'z'=16,'xl'=2,'c'=2] {'z'}, dimensions={0} | all-to-all | bytes 278528 | tf_op jit(solution)/shard_map/all_to_all | solution.py:170
  33.6 0.2 second_kernel.1
  33.7 22.1 %all_to_all.21.own_ref = bf16[32,16,384]{2,1,0:T(8,128)(2,1)S(1)} all-to-all(bf16[32,16,384]{2,1,0:T(8,128)(2,1)S(1)} %second_kernel.1), channel_id=1, replica_groups=mesh['xh'=2,'y'=8,'z'=16,'xl'=2,'c'=2] {'xh','y','xl'}, dimensions={0} | all-to-all | bytes 786432 | tf_op jit(solution)/shard_map/all_to_all | solution.py:170
  55.9 7.1 %collective-permute-start = (bf16[32,16,384]{2,1,0:T(8,128)(2,1)S(1)}, bf16[32,16,384]{2,1,0:T(8,128)(2,1)S(1)}, u32[]{:S(2)}, u32[]{:S(2)}) collective-permute-start(bf16[32,16,384]{2,1,0:T(8,128)(2,1)S(1)} %all_to_all.21.own_ref), channel_id=1, source_target_pairs={{0,1},{1,0},{2,3},{3,2},{4,5},{5,4},{6,7},{7,6},{8,9},{9,8},{10,11... | collective-permute-start | bytes 1179656 | tf_op jit(solution)/shard_map/ppermute | solution.py:174
  63.0 1.6 %own_kernel.1 = (bf16[2,256,256]{2,1,0:T(8,128)(2,1)S(1)}, bf16[16,4,16,1024]{3,2,1,0:T(8,128)(2,1)S(1)}) custom-call(bf16[32,16,384]{2,1,0:T(8,128)(2,1)S(1)} %all_to_all.21.own_ref, bf16[16,4,16,1024]{3,2,1,0:T(8,128)(2,1)} %bitcast.6), custom_call_target="tpu_custom_call" | custom-call | tf_op jit(solution)/shard_map/own_kernel/pallas_call | solution.py:158
  64.6 0.0 collective-permute-done.other_ref
  64.6 1.3 %send_kernel.1 = (bf16[32,16,256]{2,1,0:T(8,128)(2,1)S(1)}, bf16[256,256]{1,0:T(8,128)(2,1)S(1)}, bf16[1024,256]{1,0:T(8,128)(2,1)S(1)}) custom-call(s32[1]{0:T(128)} %bitcast.at_ref, bf16[32,16,384]{2,1,0:T(8,128)(2,1)S(1)} %all_to_all.21.own_ref, bf16[2,256,256]{2,1,0:T(8,128)(2,1)S(1)} %get-tuple-element.10.own_trials_ref, ...), custom_call_target="tpu_custom_call" | custom-call | tf_op jit(solution)/shard_map/send_kernel/pallas_call | solution.py:158
  65.9 2.0 %collective-permute-start.1 = (bf16[32,16,256]{2,1,0:T(8,128)(2,1)S(1)}, bf16[32,16,256]{2,1,0:T(8,128)(2,1)S(1)}, u32[]{:S(2)}, u32[]{:S(2)}) collective-permute-start(bf16[32,16,256]{2,1,0:T(8,128)(2,1)S(1)} %get-tuple-element.14), channel_id=1, source_target_pairs={{0,1},{1,0},{2,3},{3,2},{4,5},{5,4},{6,7},{7,6},{8,9},{9,8},{10,11... | collective-permute-start | bytes 786440 | tf_op jit(solution)/shard_map/ppermute | solution.py:174
  67.9 1.1 %keep_kernel.1.kept_ref = f32[32,16,256]{2,1,0:T(8,128)S(1)} custom-call(s32[1]{0:T(128)} %bitcast.at_ref, bf16[256,256]{1,0:T(8,128)(2,1)S(1)} %get-tuple-element.12.screened_ref, bf16[1024,256]{1,0:T(8,128)(2,1)S(1)} %get-tuple-element.13.trials_ref, bf16[16,4,16,1024]{3,2,1,0:T(8,128)(2,1)S(1)} %get-tuple-element.11.virtual_ref), custom_call_target="tpu_custom_call" | custom-call | tf_op jit(solution)/shard_map/keep_kernel/pallas_call | solution.py:158
  69.0 0.4 collective-permute-done.1.got_ref
  69.4 15.9 %all_to_all.22.got_ref = bf16[32,16,256]{2,1,0:T(8,128)(2,1)S(1)} all-to-all(bf16[32,16,256]{2,1,0:T(8,128)(2,1)S(1)} %add_kernel.1), channel_id=1, replica_groups=mesh['xh'=2,'y'=8,'z'=16,'xl'=2,'c'=2] {'xh','y','xl'}, dimensions={0} | all-to-all | bytes 524288 | tf_op jit(solution)/shard_map/all_to_all | solution.py:170
  85.3 0.3 fourth_kernel.1
  85.5 17.5 %all_to_all.23.got_ref = f32[16,2,128]{2,1,0:T(2,128)S(1)} all-to-all(f32[16,2,128]{2,1,0:T(2,128)S(1)} %fourth_kernel.1), channel_id=1, replica_groups=mesh['xh'=2,'y'=8,'z'=16,'xl'=2,'c'=2] {'z'}, dimensions={0} | all-to-all | bytes 32768 | tf_op jit(solution)/shard_map/all_to_all | solution.py:170
  103.0 0.9 last_kernel.1
  (1 shorter events, 0.0 us)
Async XLA Ops:
  55.9 8.7 %collective-permute-start = (bf16[32,16,384]{2,1,0:T(8,128)(2,1)S(1)}, bf16[32,16,384]{2,1,0:T(8,128)(2,1)S(1)}, u32[]{:S(2)}, u32[]{:S(2)}) collective-permute-start(bf16[32,16,384]{2,1,0:T(8,128)(2,1)S(1)} %all_to_all.21.own_ref), channel_id=1, source_target_pairs={{0,1},{1,0},{2,3},{3,2},{4,5},{5,4},{6,7},{7,6},{8,9},{9,8},{10,11... | collective-permute-start | bytes 1179656 | tf_op jit(solution)/shard_map/ppermute | solution.py:174
  65.9 3.4 %collective-permute-start.1 = (bf16[32,16,256]{2,1,0:T(8,128)(2,1)S(1)}, bf16[32,16,256]{2,1,0:T(8,128)(2,1)S(1)}, u32[]{:S(2)}, u32[]{:S(2)}) collective-permute-start(bf16[32,16,256]{2,1,0:T(8,128)(2,1)S(1)} %get-tuple-element.14), channel_id=1, source_target_pairs={{0,1},{1,0},{2,3},{3,2},{4,5},{5,4},{6,7},{7,6},{8,9},{9,8},{10,11... | collective-permute-start | bytes 786440 | tf_op jit(solution)/shard_map/ppermute | solution.py:174

commit v7 on v6

--- a/solution.py
+++ b/solution.py
@@ -35,19 +35,20 @@
     at_ref, pairs_hbm, screening_hbm, trials_hbm, out_ref, pairs_ref, screening_ref, trials_ref, columns_ref, sems
 ):
     copies = [pltpu.make_async_copy(pairs_hbm, pairs_ref, sems.at[0])]
-    for k in range(2):
-        part = pl.ds(O * 2 * k, O * 2)
-        copies.append(pltpu.make_async_copy(screening_hbm.at[:, part], screening_ref.at[:, part], sems.at[1 + k]))
-    copies.append(pltpu.make_async_copy(trials_hbm, trials_ref, sems.at[3]))
+    for k in range(8):
+        part = (pl.ds(O * (k % 4), O), pl.ds(O * 2 * (k // 4), O * 2))
+        copies.append(pltpu.make_async_copy(screening_hbm.at[part], screening_ref.at[part], sems.at[1 + k]))
+    copies.append(pltpu.make_async_copy(trials_hbm, trials_ref, sems.at[9]))
     for copy in copies:
         copy.start()
     copies[0].wait()
     for k in range(2):
-        copies[1 + k].wait()
+        for r in range(4):
+            copies[1 + 4 * k + r].wait()
         columns = dot(pairs_ref[...], screening_ref[:, O * 2 * k : O * 2 * (k + 1)], 1, 0).T
         for w in range(8):
             columns_ref[pl.ds(STEP * (8 * k + w), 64), :] = columns[64 * w : 64 * (w + 1), :]
-    copies[3].wait()
+    copies[9].wait()
     mine = iota((BLK, O), 0) == at_ref[0]
     row = jnp.sum(jnp.where(mine, trials_ref[...].astype(F32), 0.0), 0, keepdims=True)
     tail = jnp.where(iota((2, 128), 0) == 0, row[:, :128], row[:, 128:]).astype(BF)
@@ -73,23 +74,34 @@
     return [dot(flip, tile, 1, 0).astype(BF) for tile in tiles]
 
 
-def own_kernel(own_ref, virtual_hbm, trials_ref, virtual_ref, sem):
-    copy = pltpu.make_async_copy(virtual_hbm, virtual_ref, sem)
-    copy.start()
-    trials_ref[0], trials_ref[1] = ordered(own_ref)
-    copy.wait()
+def place(ref, c, trials_ref):
+    for x, tile in enumerate(ordered(ref)):
+        for z in range(Z):
+            start = pl.multiple_of(64 * z + 32 * x + BLK * c, BLK)
+            trials_ref[pl.ds(start, BLK), :] = tile[W * z : W * (z + 1), :]
+
+
+def own_kernel(at_ref, own_ref, virtual_hbm, trials_ref, virtual_ref, sems):
+    copies = []
+    for k in range(4):
+        part = pl.ds(4 * k, 4)
+        copies.append(pltpu.make_async_copy(virtual_hbm.at[part], virtual_ref.at[part], sems.at[k]))
+        copies[k].start()
+    place(own_ref, at_ref[0], trials_ref)
+    for copy in copies:
+        copy.wait()
 
 
 def partial(of, screened_ref, trials_ref, virtual_ref, out_ref):
+    rows = jnp.concatenate([virtual_ref[:, 2 * x + of].reshape(O, V) for x in range(2)], 0)
+    halves = dot(rows, trials_ref[...], 1, 0).astype(BF)
     for x in range(2):
-        rows = virtual_ref[:, 2 * x + of].reshape(O, V)
-        halves = dot(rows, trials_ref[...], 1, 0).astype(BF)
-        part = dot(screened_ref[...], halves, 1, 1).astype(out_ref.dtype)
+        part = dot(screened_ref[...], halves[O * x : O * (x + 1), :], 1, 1).astype(out_ref.dtype)
         for w in range(W):
             out_ref[2 * w + x] = part[BLK * w : BLK * (w + 1), :]
 
 
-def send_kernel(at_ref, own_ref, own_trials_ref, other_ref, virtual_ref, send_ref, screened_ref, trials_ref):
+def send_kernel(at_ref, own_ref, part_ref, other_ref, virtual_ref, send_ref, screened_ref, trials_ref):
     core = at_ref[0]
     here = iota((BLK, 128), 1) // 64 == core
     for w in range(W):
@@ -97,11 +109,7 @@
             moved = pltpu.roll(other_ref[2 * w + x, :, :128].astype(F32), 64, 1)
             tile = jnp.where(here, own_ref[2 * w + x, :, :128].astype(F32), moved)
             screened_ref[BLK * w : BLK * (w + 1), 128 * x : 128 * (x + 1)] = tile.astype(BF)
-    for tiles, c in (((own_trials_ref[0], own_trials_ref[1]), core), (ordered(other_ref), 1 - core)):
-        for x in range(2):
-            for z in range(Z):
-                start = pl.multiple_of(64 * z + 32 * x + BLK * c, BLK)
-                trials_ref[pl.ds(start, BLK), :] = tiles[x][W * z : W * (z + 1), :]
+    place(other_ref, 1 - core, trials_ref)
     partial(1 - core, screened_ref, trials_ref, virtual_ref, send_ref)
 
 
@@ -150,7 +158,7 @@
     return pltpu.VMEM(shape, dtype)
 
 
-def call(body, outs, *args, scratch=(), limit=24 << 20, hbm=()):
+def call(body, outs, *args, scratch=(), limit=24 << 20, hbm=(), alias={}):
     vmem = pl.BlockSpec(memory_space=pltpu.VMEM)
     specs = [pl.BlockSpec(memory_space=pltpu.SMEM) if a.dtype == jnp.int32 else vmem for a in args]
     for at in hbm:
@@ -162,6 +170,7 @@
         out_specs=jax.tree.map(lambda o: vmem, outs),
         scratch_shapes=scratch,
         compiler_params=pltpu.CompilerParams(vmem_limit_bytes=limit),
+        input_output_aliases=alias,
         name=body.__name__,
     )(*args)
 
@@ -189,7 +198,7 @@
             pltpu.VMEM((V, V), BF),
             pltpu.VMEM((BLK, O), BF),
             pltpu.VMEM((W * STEP, 64), F32),
-            pltpu.SemaphoreType.DMA((4,)),
+            pltpu.SemaphoreType.DMA((10,)),
         ],
         hbm=(1, 2, 3),
     )
@@ -199,11 +208,12 @@
     other = across(own)
     own_trials, virtual = call(
         own_kernel,
-        (vmem_out((2, O, O), BF), vmem_out((Z, 4, BLK, V), BF)),
+        (vmem_out((V, O), BF), vmem_out((Z, 4, BLK, V), BF)),
+        core,
         own,
         in_hbm(virtual_integrals.reshape(Z, 4, BLK, V)),
-        scratch=[pltpu.SemaphoreType.DMA(())],
-        hbm=(1,),
+        scratch=[pltpu.SemaphoreType.DMA((4,))],
+        hbm=(2,),
     )
     sent, screened, whole = call(
         send_kernel,
@@ -213,6 +223,7 @@
         own_trials,
         other,
         virtual,
+        alias={2: 2},
     )
     got = across(sent)
     kept = call(keep_kernel, vmem_out((2 * W, BLK, O), F32), core, screened, whole, virtual)

time: 105 us -> 105 us (level)
  transfers between devices with their start and end apart: 2 -> 2, of which waited for: 1 -> 1; matrix products, arithmetic and copies ran while one was open for 0% -> 0% of each run, Pallas kernels for 3% -> 2%
where the time goes in v7:
time: 105 us; the launch traced here: 104 us
  blocking collectives  86.7 us (83%)
  starting transfers between devices  9.07 us (9%)
  Pallas kernels  7.01 us (7%)
    all_to_all x4, blocking collectives, swap(): return in_vmem(lax.all_to_all(v, axis, 0, 0, tiled=True))  86.7 us
    ppermute x2, starting transfers between devices, across(): return in_vmem(lax.ppermute(v, 'c', [(0, 1), (1, 0)]))  9.07 us
    pallas_call x8, Pallas kernels, call(): pl.pallas_call(body, out_shape=outs, in_specs=specs, out_specs=jax.tree.m...  7.01 us
  transfers between devices with their start and end apart: 2, of which 1 were waited for; matrix products, arithmetic and copies ran while one was open for 0% of the time, Pallas kernels for 2%

profile of v7, /device:TPU:1, one launch (start us, length us, event | category | flops | bytes accessed | tf_op | source)
XLA Modules:
  0.0 103.6 jit_solution(11676165376419690594)
XLA Ops:
  0.0 2.4 %first_kernel.1 = bf16[16,17,2,128]{3,2,1,0:T(2,128)(2,1)S(1)} custom-call(s32[1]{0:T(128)} %bitcast.1.at_ref, bf16[64,1024]{1,0:T(8,128)(2,1)} %pairs_hbm.1, bf16[1024,1024]{1,0:T(8,128)(2,1)} %screening_hbm.1, bf16[16,256]{1,0:T(8,128)(2,1)} %bitcast.7), custom_call_target="tpu_custom_call" | custom-call | tf_op jit(solution)/shard_map/first_kernel/pallas_call | solution.py:166
  2.4 31.2 %all_to_all.20.got_ref = bf16[16,17,2,128]{3,2,1,0:T(2,128)(2,1)S(1)} all-to-all(bf16[16,17,2,128]{3,2,1,0:T(2,128)(2,1)S(1)} %first_kernel.1), channel_id=1, replica_groups=mesh['xh'=2,'y'=8,'z'=16,'xl'=2,'c'=2] {'z'}, dimensions={0} | all-to-all | bytes 278528 | tf_op jit(solution)/shard_map/all_to_all | solution.py:179
  33.6 0.2 second_kernel.1
  33.7 22.2 %all_to_all.21.own_ref = bf16[32,16,384]{2,1,0:T(8,128)(2,1)S(1)} all-to-all(bf16[32,16,384]{2,1,0:T(8,128)(2,1)S(1)} %second_kernel.1), channel_id=1, replica_groups=mesh['xh'=2,'y'=8,'z'=16,'xl'=2,'c'=2] {'xh','y','xl'}, dimensions={0} | all-to-all | bytes 786432 | tf_op jit(solution)/shard_map/all_to_all | solution.py:179
  55.9 7.1 %collective-permute-start = (bf16[32,16,384]{2,1,0:T(8,128)(2,1)S(1)}, bf16[32,16,384]{2,1,0:T(8,128)(2,1)S(1)}, u32[]{:S(2)}, u32[]{:S(2)}) collective-permute-start(bf16[32,16,384]{2,1,0:T(8,128)(2,1)S(1)} %all_to_all.21.own_ref), channel_id=1, source_target_pairs={{0,1},{1,0},{2,3},{3,2},{4,5},{5,4},{6,7},{7,6},{8,9},{9,8},{10,11... | collective-permute-start | bytes 1179656 | tf_op jit(solution)/shard_map/ppermute | solution.py:183
  63.0 1.6 %own_kernel.1 = (bf16[1024,256]{1,0:T(8,128)(2,1)S(1)}, bf16[16,4,16,1024]{3,2,1,0:T(8,128)(2,1)S(1)}) custom-call(s32[1]{0:T(128)} %bitcast.at_ref, bf16[32,16,384]{2,1,0:T(8,128)(2,1)S(1)} %all_to_all.21.own_ref, bf16[16,4,16,1024]{3,2,1,0:T(8,128)(2,1)} %bitcast.6), custom_call_target="tpu_custom_call" | custom-call | tf_op jit(solution)/shard_map/own_kernel/pallas_call | solution.py:166
  64.5 0.0 collective-permute-done.other_ref
  64.6 1.0 send_kernel.1
  65.6 2.0 %collective-permute-start.1 = (bf16[32,16,256]{2,1,0:T(8,128)(2,1)S(1)}, bf16[32,16,256]{2,1,0:T(8,128)(2,1)S(1)}, u32[]{:S(2)}, u32[]{:S(2)}) collective-permute-start(bf16[32,16,256]{2,1,0:T(8,128)(2,1)S(1)} %get-tuple-element.14), channel_id=1, source_target_pairs={{0,1},{1,0},{2,3},{3,2},{4,5},{5,4},{6,7},{7,6},{8,9},{9,8},{10,11... | collective-permute-start | bytes 786440 | tf_op jit(solution)/shard_map/ppermute | solution.py:183
  67.6 0.7 keep_kernel.1.kept_ref
  68.3 0.7 collective-permute-done.1.got_ref
  69.1 15.9 %all_to_all.22.got_ref = bf16[32,16,256]{2,1,0:T(8,128)(2,1)S(1)} all-to-all(bf16[32,16,256]{2,1,0:T(8,128)(2,1)S(1)} %add_kernel.1), channel_id=1, replica_groups=mesh['xh'=2,'y'=8,'z'=16,'xl'=2,'c'=2] {'xh','y','xl'}, dimensions={0} | all-to-all | bytes 524288 | tf_op jit(solution)/shard_map/all_to_all | solution.py:179
  84.9 0.3 fourth_kernel.1
  85.2 17.5 %all_to_all.23.got_ref = f32[16,2,128]{2,1,0:T(2,128)S(1)} all-to-all(f32[16,2,128]{2,1,0:T(2,128)S(1)} %fourth_kernel.1), channel_id=1, replica_groups=mesh['xh'=2,'y'=8,'z'=16,'xl'=2,'c'=2] {'z'}, dimensions={0} | all-to-all | bytes 32768 | tf_op jit(solution)/shard_map/all_to_all | solution.py:179
  102.7 0.9 last_kernel.1
  (1 shorter events, 0.0 us)
Async XLA Ops:
  55.9 8.6 %collective-permute-start = (bf16[32,16,384]{2,1,0:T(8,128)(2,1)S(1)}, bf16[32,16,384]{2,1,0:T(8,128)(2,1)S(1)}, u32[]{:S(2)}, u32[]{:S(2)}) collective-permute-start(bf16[32,16,384]{2,1,0:T(8,128)(2,1)S(1)} %all_to_all.21.own_ref), channel_id=1, source_target_pairs={{0,1},{1,0},{2,3},{3,2},{4,5},{5,4},{6,7},{7,6},{8,9},{9,8},{10,11... | collective-permute-start | bytes 1179656 | tf_op jit(solution)/shard_map/ppermute | solution.py:183
  65.6 3.4 %collective-permute-start.1 = (bf16[32,16,256]{2,1,0:T(8,128)(2,1)S(1)}, bf16[32,16,256]{2,1,0:T(8,128)(2,1)S(1)}, u32[]{:S(2)}, u32[]{:S(2)}) collective-permute-start(bf16[32,16,256]{2,1,0:T(8,128)(2,1)S(1)} %get-tuple-element.14), channel_id=1, source_target_pairs={{0,1},{1,0},{2,3},{3,2},{4,5},{5,4},{6,7},{7,6},{8,9},{9,8},{10,11... | collective-permute-start | bytes 786440 | tf_op jit(solution)/shard_map/ppermute | solution.py:183

commit v8 on v7

--- a/solution.py
+++ b/solution.py
@@ -81,15 +81,8 @@
             trials_ref[pl.ds(start, BLK), :] = tile[W * z : W * (z + 1), :]
 
 
-def own_kernel(at_ref, own_ref, virtual_hbm, trials_ref, virtual_ref, sems):
-    copies = []
-    for k in range(4):
-        part = pl.ds(4 * k, 4)
-        copies.append(pltpu.make_async_copy(virtual_hbm.at[part], virtual_ref.at[part], sems.at[k]))
-        copies[k].start()
+def own_kernel(at_ref, own_ref, trials_ref):
     place(own_ref, at_ref[0], trials_ref)
-    for copy in copies:
-        copy.wait()
 
 
 def partial(of, screened_ref, trials_ref, virtual_ref, out_ref):
@@ -206,15 +199,8 @@
     sent = call(second_kernel, vmem_out((2 * W, Z, 384), BF), got, scratch=[pltpu.VMEM((Z * 34, 128), F32)])
     own = swap(sent, XY)
     other = across(own)
-    own_trials, virtual = call(
-        own_kernel,
-        (vmem_out((V, O), BF), vmem_out((Z, 4, BLK, V), BF)),
-        core,
-        own,
-        in_hbm(virtual_integrals.reshape(Z, 4, BLK, V)),
-        scratch=[pltpu.SemaphoreType.DMA((4,))],
-        hbm=(2,),
-    )
+    own_trials = call(own_kernel, vmem_out((V, O), BF), core, own)
+    virtual = in_vmem(virtual_integrals.reshape(Z, 4, BLK, V))
     sent, screened, whole = call(
         send_kernel,
         (vmem_out((2 * W, BLK, O), BF), vmem_out((O, O), BF), vmem_out((V, O), BF)),

time: 105 us -> 105 us (level)
  Pallas kernels: 7.01 us -> 5.81 us
    pallas_call x8, Pallas kernels: 7.01 us -> 5.81 us  [call(): pl.pallas_call(body, out_shape=outs, in_specs=specs, out_specs=jax.tree.m...]
  transfers between devices with their start and end apart: 2 -> 2, of which waited for: 1 -> 2; matrix products, arithmetic and copies ran while one was open for 0% -> 0% of each run, Pallas kernels for 2% -> 1%
where the time goes in v8:
time: 105 us; the launch traced here: 103 us
  blocking collectives  86.7 us (83%)
  starting transfers between devices  9.33 us (9%)
  Pallas kernels  5.81 us (6%)
  waiting for transfers between devices  1.53 us (1%)
    all_to_all x4, blocking collectives, swap(): return in_vmem(lax.all_to_all(v, axis, 0, 0, tiled=True))  86.7 us
    ppermute x2, starting transfers between devices, across(): return in_vmem(lax.ppermute(v, 'c', [(0, 1), (1, 0)]))  9.33 us
    pallas_call x8, Pallas kernels, call(): pl.pallas_call(body, out_shape=outs, in_specs=specs, out_specs=jax.tree.m...  5.81 us
  transfers between devices with their start and end apart: 2, of which 2 were waited for; matrix products, arithmetic and copies ran while one was open for 0% of the time, Pallas kernels for 1%

profile of v8, /device:TPU:1, one launch (start us, length us, event | category | flops | bytes accessed | tf_op | source)
XLA Modules:
  0.0 103.4 jit_solution(4383702786053686289)
XLA Ops:
  0.0 0.0 copy-start
  0.0 2.5 %first_kernel.1 = bf16[16,17,2,128]{3,2,1,0:T(2,128)(2,1)S(1)} custom-call(s32[1]{0:T(128)} %bitcast.1.at_ref, bf16[64,1024]{1,0:T(8,128)(2,1)} %pairs_hbm.1, bf16[1024,1024]{1,0:T(8,128)(2,1)} %screening_hbm.1, bf16[16,256]{1,0:T(8,128)(2,1)} %bitcast.8), custom_call_target="tpu_custom_call" | custom-call | tf_op jit(solution)/shard_map/first_kernel/pallas_call | solution.py:159
  2.5 31.2 %all_to_all.20.got_ref = bf16[16,17,2,128]{3,2,1,0:T(2,128)(2,1)S(1)} all-to-all(bf16[16,17,2,128]{3,2,1,0:T(2,128)(2,1)S(1)} %first_kernel.1), channel_id=1, replica_groups=mesh['xh'=2,'y'=8,'z'=16,'xl'=2,'c'=2] {'z'}, dimensions={0} | all-to-all | bytes 278528 | tf_op jit(solution)/shard_map/all_to_all | solution.py:172
  33.7 0.2 second_kernel.1
  33.9 22.2 %all_to_all.21.own_ref = bf16[32,16,384]{2,1,0:T(8,128)(2,1)S(1)} all-to-all(bf16[32,16,384]{2,1,0:T(8,128)(2,1)S(1)} %second_kernel.1), channel_id=1, replica_groups=mesh['xh'=2,'y'=8,'z'=16,'xl'=2,'c'=2] {'xh','y','xl'}, dimensions={0} | all-to-all | bytes 786432 | tf_op jit(solution)/shard_map/all_to_all | solution.py:172
  56.0 7.1 %collective-permute-start = (bf16[32,16,384]{2,1,0:T(8,128)(2,1)S(1)}, bf16[32,16,384]{2,1,0:T(8,128)(2,1)S(1)}, u32[]{:S(2)}, u32[]{:S(2)}) collective-permute-start(bf16[32,16,384]{2,1,0:T(8,128)(2,1)S(1)} %all_to_all.21.own_ref), channel_id=1, source_target_pairs={{0,1},{1,0},{2,3},{3,2},{4,5},{5,4},{6,7},{7,6},{8,9},{9,8},{10,11... | collective-permute-start | bytes 1179656 | tf_op jit(solution)/shard_map/ppermute | solution.py:176
  63.1 0.2 own_kernel.1.part_ref
  63.4 1.1 %collective-permute-done.other_ref = bf16[32,16,384]{2,1,0:T(8,128)(2,1)S(1)} collective-permute-done((bf16[32,16,384]{2,1,0:T(8,128)(2,1)S(1)}, bf16[32,16,384]{2,1,0:T(8,128)(2,1)S(1)}, u32[]{:S(2)}, u32[]{:S(2)}) %collective-permute-start) | collective-permute-done | bytes 393248 | tf_op jit(solution)/shard_map/ppermute | solution.py:176
  64.4 0.0 copy-done
  64.4 1.0 send_kernel.1
  65.5 2.3 %collective-permute-start.1 = (bf16[32,16,256]{2,1,0:T(8,128)(2,1)S(1)}, bf16[32,16,256]{2,1,0:T(8,128)(2,1)S(1)}, u32[]{:S(2)}, u32[]{:S(2)}) collective-permute-start(bf16[32,16,256]{2,1,0:T(8,128)(2,1)S(1)} %get-tuple-element.10), channel_id=1, source_target_pairs={{0,1},{1,0},{2,3},{3,2},{4,5},{5,4},{6,7},{7,6},{8,9},{9,8},{10,11... | collective-permute-start | bytes 786440 | tf_op jit(solution)/shard_map/ppermute | solution.py:176
  67.8 0.7 keep_kernel.1.kept_ref
  68.4 0.5 collective-permute-done.1.got_ref
  68.9 15.9 %all_to_all.22.got_ref = bf16[32,16,256]{2,1,0:T(8,128)(2,1)S(1)} all-to-all(bf16[32,16,256]{2,1,0:T(8,128)(2,1)S(1)} %add_kernel.1), channel_id=1, replica_groups=mesh['xh'=2,'y'=8,'z'=16,'xl'=2,'c'=2] {'xh','y','xl'}, dimensions={0} | all-to-all | bytes 524288 | tf_op jit(solution)/shard_map/all_to_all | solution.py:172
  84.8 0.3 fourth_kernel.1
  85.1 17.4 %all_to_all.23.got_ref = f32[16,2,128]{2,1,0:T(2,128)S(1)} all-to-all(f32[16,2,128]{2,1,0:T(2,128)S(1)} %fourth_kernel.1), channel_id=1, replica_groups=mesh['xh'=2,'y'=8,'z'=16,'xl'=2,'c'=2] {'z'}, dimensions={0} | all-to-all | bytes 32768 | tf_op jit(solution)/shard_map/all_to_all | solution.py:172
  102.5 0.9 last_kernel.1
  (1 shorter events, 0.0 us)
Async XLA Ops:
  0.0 64.4 %copy-start = (bf16[1,1024,1024]{2,1,0:T(8,128)(2,1)S(1)}, bf16[1,1024,1024]{2,1,0:T(8,128)(2,1)}, u32[]{:S(2)}) copy-start(bf16[1,1024,1024]{2,1,0:T(8,128)(2,1)} %param.6) | copy-start | bytes 6291460
  56.0 8.4 %collective-permute-start = (bf16[32,16,384]{2,1,0:T(8,128)(2,1)S(1)}, bf16[32,16,384]{2,1,0:T(8,128)(2,1)S(1)}, u32[]{:S(2)}, u32[]{:S(2)}) collective-permute-start(bf16[32,16,384]{2,1,0:T(8,128)(2,1)S(1)} %all_to_all.21.own_ref), channel_id=1, source_target_pairs={{0,1},{1,0},{2,3},{3,2},{4,5},{5,4},{6,7},{7,6},{8,9},{9,8},{10,11... | collective-permute-start | bytes 1179656 | tf_op jit(solution)/shard_map/ppermute | solution.py:176
  65.5 3.4 %collective-permute-start.1 = (bf16[32,16,256]{2,1,0:T(8,128)(2,1)S(1)}, bf16[32,16,256]{2,1,0:T(8,128)(2,1)S(1)}, u32[]{:S(2)}, u32[]{:S(2)}) collective-permute-start(bf16[32,16,256]{2,1,0:T(8,128)(2,1)S(1)} %get-tuple-element.10), channel_id=1, source_target_pairs={{0,1},{1,0},{2,3},{3,2},{4,5},{5,4},{6,7},{7,6},{8,9},{9,8},{10,11... | collective-permute-start | bytes 786440 | tf_op jit(solution)/shard_map/ppermute | solution.py:176
